TPU v7x, 128 devices: a whole 4x4x4 slice. The times are simulated.
128 devices in a mesh: gx: 8 (over x, z_lo), gy: 16 (over z_hi, y, core).
Axes of the slice: x: 4, y: 4, z: 4 (z_hi: 2, z_lo: 2; z = z_hi * 2 + z_lo), core: 2. Of those that a mesh axis runs over, the one named last changes fastest.
Arguments:
- state: float32 [8, 8, 128, 2048], P(None, None, 'gx', 'gy'), may hold values from -3 to 3
- residual: float32 [128], replicated, may hold values from -2.5 to 2.5
- shift_rows: int32 [128], P('gx'), may hold values from 0 to 2047
- shear_offset: int32 [1], replicated, may hold values from 0 to 2047
Outputs:
- evolved: float32 [8, 8, 128, 2048], P(None, None, 'gx', 'gy')
Inputs may be any that keep to these rules, and one draw needn't show every extreme that they name: `shift_rows`: each row's whole-cell displacement; it wraps around the 2048 azimuthal cells. `shear_offset`: whole-cell offset of the sheared radial boundary.
All inputs are finite; a program needn't handle non-finite values.
Results may differ from a plain program's by a relative error of at most 0.00002.
Values sent between devices are 32-bit elements; how exact they have to be, the bound alone decides.
No kernel may reach another device: no remote copies, remote signals or barrier semaphores. Data moves between devices by JAX's collectives and lax.ppermute only.
A program may use at most 128 MiB of HBM per device.

v0:
```python
import jax
import jax.numpy as jnp
from jax import lax
from jax.experimental import pallas as pl
from jax.experimental.pallas import tpu as pltpu
from jax.sharding import PartitionSpec as P

time_step = 0.2
viscous = 0.1
resist = 0.1
sound_sq = 1.0
rotation = 0.5
shear_rate = 1.5

LANES = 128
DEPTH = 2
STRIP = 4 * DEPTH


def passed_along(value, axis, steps):
    count = lax.axis_size(axis)
    pairs = [(source, (source + steps) % count) for source in range(count)]
    return lax.ppermute(value, axis, pairs)


def turn_lines(groups, rows, planes):
    own = rows * planes
    ghost = DEPTH * planes
    total = own + 2 * ghost
    wide = rows + 2 * DEPTH
    pitch = wide + 2

    def kernel(shifts, mine, low, high, out, lines, sems):
        copies = []
        for part, (source, start, size) in enumerate(
            ((mine, 0, own), (low, own, ghost), (high, own + ghost, ghost))
        ):
            for turn, (first, count, target) in enumerate(
                ((0, groups, 1), (0, groups, groups + 1), (groups - 1, 1, 0))
            ):
                copies.append(
                    pltpu.make_async_copy(
                        source.at[pl.ds(first, count)],
                        lines.at[pl.ds(target, count), pl.ds(start, size)],
                        sems.at[part, turn],
                    )
                )
        for copy in copies:
            copy.start()
        for copy in copies:
            copy.wait()
        flat = lines.reshape((2 * groups + 1) * total, LANES)
        lane = lax.broadcasted_iota(jnp.int32, (groups, LANES), 1)
        strips = [[jnp.zeros((groups, LANES), jnp.float32) for _ in range(planes)] for _ in range(2)]
        for row in range(wide):
            amount = shifts[row]
            block = (groups - amount // LANES) % groups
            part = amount % LANES
            keep = lane < LANES - part
            edge = ((lane + part) & (LANES - 1)) < 2 * DEPTH
            place = row // 2
            strip_turn = (part + 2 * DEPTH + STRIP * place) % LANES
            in_place = (lane >= STRIP * place) & (lane < STRIP * (place + 1))
            for plane in range(planes):
                if row < DEPTH:
                    line = own + plane * DEPTH + row
                elif row < DEPTH + rows:
                    line = plane * rows + row - DEPTH
                else:
                    line = own + ghost + plane * DEPTH + row - DEPTH - rows
                before, here, after = (
                    flat[pl.ds((block + ahead_by) * total + line, groups, stride=total), :]
                    for ahead_by in range(3)
                )
                window = jnp.where(keep, here, before)
                out[pl.ds(plane * pitch + row, groups, stride=planes * pitch), :] = pltpu.roll(
                    window, part, 1
                )
                rim = jnp.where(edge, jnp.where(keep, after, here), window)
                strips[row % 2][plane] = jnp.where(
                    in_place, pltpu.roll(rim, strip_turn, 1), strips[row % 2][plane]
                )
        for parity in range(2):
            for plane in range(planes):
                out[pl.ds(plane * pitch + wide + parity, groups, stride=planes * pitch), :] = strips[
                    parity
                ][plane]

    return pl.pallas_call(
        kernel,
        in_specs=[pl.BlockSpec(memory_space=pltpu.SMEM)] + [pl.BlockSpec(memory_space=pl.ANY)] * 3,
        out_shape=jax.ShapeDtypeStruct((groups * planes * pitch, LANES), jnp.float32),
        out_specs=pl.BlockSpec(memory_space=pltpu.VMEM),
        scratch_shapes=[
            pltpu.VMEM((2 * groups + 1, total, LANES), jnp.float32),
            pltpu.SemaphoreType.DMA((3, 3)),
        ],
        compiler_params=pltpu.CompilerParams(vmem_limit_bytes=24 * 1024 * 1024),
        name="turn_lines",
    )


def y_up(tile):
    return pltpu.roll(tile, LANES - 1, 1)


def y_dn(tile):
    return pltpu.roll(tile, 1, 1)


def z_up(tile):
    return pltpu.roll(tile, tile.shape[0] - 1, 0)


def z_dn(tile):
    return pltpu.roll(tile, 1, 0)


def radial_edges(prev, here, drift_prev, drift):
    _, vel_x, _, vel_z, _, mag_x, mag_y, mag_z = here
    two_x = vel_x + prev[1]
    two_z = vel_z + prev[3]
    two_w = drift + drift_prev
    mag_x_y = y_dn(mag_x)
    mag_x_z = z_dn(mag_x)
    emf_z = 0.125 * (
        (two_w + y_dn(two_w)) * (mag_x + mag_x_y) - (two_x + y_dn(two_x)) * (mag_y + prev[6])
    ) + resist * ((mag_y - prev[6]) - (mag_x - mag_x_y))
    emf_y = 0.125 * (
        (two_x + z_dn(two_x)) * (mag_z + prev[7]) - (two_z + z_dn(two_z)) * (mag_x + mag_x_z)
    ) + resist * ((mag_x - mag_x_z) - (mag_z - prev[7]))
    return emf_z, emf_y


def row_rates(prev, here, after, residual, edges, edges_after):
    log_rho, vel_x, vel_y, vel_z, entropy, mag_x, mag_y, mag_z = here
    drift = vel_y + residual
    half_x = 0.5 * vel_x
    half_w = 0.5 * drift
    half_z = 0.5 * vel_z

    def moved_by(index):
        center = here[index]
        fore, back = after[index], prev[index]
        left, right = y_dn(center), y_up(center)
        under, over = z_dn(center), z_up(center)
        d_x, d_y, d_z = fore - back, right - left, over - under
        total = ((fore + back) + (left + right)) + (under + over)
        rate = viscous * total - (6.0 * viscous) * center
        rate = rate - (half_x * d_x + half_w * d_y + half_z * d_z)
        return rate, d_x, d_y, d_z, left

    rate_l, l_x, l_y, l_z, _ = moved_by(0)
    rate_vx, vx_x, _, _, _ = moved_by(1)
    rate_vy, _, vy_y, _, vy_left = moved_by(2)
    rate_vz, _, _, vz_z, vz_left = moved_by(3)
    rate_s, s_x, s_y, s_z, _ = moved_by(4)

    two_bx = mag_x + after[5]
    two_by = mag_y + y_up(mag_y)
    two_bz = mag_z + z_up(mag_z)
    two_bx_left = y_dn(two_bx)
    diff_y = after[6] - prev[6]
    diff_z = after[7] - prev[7]
    cur_x = (y_up(two_bz) - y_dn(two_bz)) - (z_up(two_by) - z_dn(two_by))
    cur_y = (z_up(two_bx) - z_dn(two_bx)) - (diff_z + z_up(diff_z))
    cur_z = (diff_y + y_up(diff_y)) - (y_up(two_bx) - two_bx_left)
    inverse = jnp.exp(-log_rho)
    eighth = 0.125 * inverse
    rate_l = rate_l - 0.5 * (vx_x + vy_y + vz_z)
    rate_vx = (
        rate_vx
        - (0.5 * sound_sq) * (l_x + s_x)
        + eighth * (cur_y * two_bz - cur_z * two_by)
        + (2.0 * rotation) * vel_y
    )
    rate_vy = (
        rate_vy
        - (0.5 * sound_sq) * (l_y + s_y)
        + eighth * (cur_z * two_bx - cur_x * two_bz)
        - ((2.0 - shear_rate) * rotation) * vel_x
    )
    rate_vz = (
        rate_vz
        - (0.5 * sound_sq) * (l_z + s_z)
        + eighth * (cur_x * two_by - cur_y * two_bx)
    )
    rate_s = rate_s + (resist * 0.0625) * inverse * (cur_x * cur_x + cur_y * cur_y + cur_z * cur_z)

    emf_z, emf_y = edges
    emf_z_after, emf_y_after = edges_after
    pair_w = drift + (vy_left + residual_left(residual))
    pair_z = vel_z + vz_left
    mag_z_y = y_dn(mag_z)
    mag_y_z = z_dn(mag_y)
    emf_x = 0.125 * (
        (pair_z + z_dn(pair_z)) * (mag_y + mag_y_z) - (pair_w + z_dn(pair_w)) * (mag_z + mag_z_y)
    ) + resist * ((mag_z - mag_z_y) - (mag_y - mag_y_z))
    rate_bx = (emf_z - y_up(emf_z)) + (z_up(emf_y) - emf_y)
    rate_by = (
        (emf_x - z_up(emf_x))
        + (emf_z_after - emf_z)
        - (0.25 * shear_rate * rotation) * (two_bx + two_bx_left)
    )
    rate_bz = (emf_y - emf_y_after) + (y_up(emf_x) - emf_x)
    return [rate_l, rate_vx, rate_vy, rate_vz, rate_s, rate_bx, rate_by, rate_bz]


def residual_left(residual):
    return residual


def two_sections(fields, depth, rows):
    wide = rows + 2 * DEPTH
    pitch = wide + 2
    strip_at = wide

    def kernel(residual, source, out, moved, first, drift_rows, ends):
        lane = lax.broadcasted_iota(jnp.int32, (depth, LANES), 1)

        def widen_strips(ref):
            for field in range(fields):
                even = ref[field, strip_at + 1]
                odd = ref[field, strip_at + 2]
                ref[field, strip_at] = pltpu.roll(odd, STRIP, 1)
                ref[field, strip_at + 3] = pltpu.roll(even, LANES - STRIP, 1)

        strip_drift = [jnp.zeros((depth, LANES), jnp.float32) for _ in range(2)]
        for row in range(wide):
            value = jnp.full((depth, LANES), residual[row], jnp.float32)
            drift_rows[row] = value
            strip_drift[row % 2] = jnp.where(lane // STRIP == row // 2, value, strip_drift[row % 2])
        drift_rows[strip_at] = pltpu.roll(strip_drift[1], STRIP, 1)
        drift_rows[strip_at + 1] = strip_drift[0]
        drift_rows[strip_at + 2] = strip_drift[1]
        drift_rows[strip_at + 3] = pltpu.roll(strip_drift[0], LANES - STRIP, 1)
        for field in range(fields):
            for row in range(pitch):
                moved[field, row if row < wide else row + 1] = source[
                    pl.ds(field * depth * pitch + row, depth, stride=pitch), :
                ]
        widen_strips(moved)

        def row_of(ref, row):
            return [ref[field, row] for field in range(fields)]

        def edges_of(ref, row):
            prev, here = row_of(ref, row - 1), row_of(ref, row)
            return radial_edges(
                prev, here, prev[2] + drift_rows[row - 1], here[2] + drift_rows[row]
            )

        def step(ref, row, edges):
            prev, here, after = row_of(ref, row - 1), row_of(ref, row), row_of(ref, row + 1)
            edges_after = radial_edges(
                here, after, here[2] + drift_rows[row], after[2] + drift_rows[row + 1]
            )
            rate = row_rates(prev, here, after, drift_rows[row], edges, edges_after)
            return [a + time_step * b for a, b in zip(here, rate)], edges_after

        def first_row(row, edges):
            result, edges = step(moved, row, edges)
            for field in range(fields):
                first[field, row] = result[field]
            return edges

        edges = edges_of(moved, strip_at + 1)
        for row in (strip_at + 1, strip_at + 2):
            edges = first_row(row, edges)
        widen_strips(first)
        lax.fori_loop(1, wide - 1, first_row, edges_of(moved, 1))

        edges = edges_of(first, strip_at + 1)
        for parity in range(2):
            result, edges = step(first, strip_at + 1 + parity, edges)
            for field in range(fields):
                ends[field, parity] = 0.5 * (moved[field, strip_at + 1 + parity] + result[field])

        def second_row(row, edges):
            result, edges = step(first, row, edges)
            place = row // 2
            turn = (LANES - 3 * DEPTH - STRIP * place) % LANES
            for field in range(fields):
                whole = 0.5 * (moved[field, row] + result[field])
                end = pltpu.roll(ends[field, row % 2], turn, 1)
                out[pl.ds(field * depth * rows + row - DEPTH, depth, stride=rows), :] = jnp.where(
                    lane < LANES - 2 * DEPTH, pltpu.roll(whole, LANES - DEPTH, 1), end
                )
            return edges

        lax.fori_loop(DEPTH, wide - DEPTH, second_row, edges_of(first, DEPTH))

    return pl.pallas_call(
        kernel,
        in_specs=[pl.BlockSpec(memory_space=pltpu.SMEM), pl.BlockSpec(memory_space=pltpu.VMEM)],
        out_shape=jax.ShapeDtypeStruct((fields * depth * rows, LANES), jnp.float32),
        out_specs=pl.BlockSpec(memory_space=pltpu.VMEM),
        scratch_shapes=[
            pltpu.VMEM((fields, wide + 4, depth, LANES), jnp.float32),
            pltpu.VMEM((fields, wide + 4, depth, LANES), jnp.float32),
            pltpu.VMEM((wide + 4, depth, LANES), jnp.float32),
            pltpu.VMEM((fields, 2, depth, LANES), jnp.float32),
        ],
        compiler_params=pltpu.CompilerParams(vmem_limit_bytes=24 * 1024 * 1024),
        name="two_sections",
    )


def local(state, residual, shift_rows, shear_offset):
    fields, depth, rows, cols = state.shape
    groups = lax.axis_size("gy")
    radial_count = lax.axis_size("gx")
    row_dev = lax.axis_index("gx")
    cells_y = cols * groups
    planes = fields * depth // groups
    offset = shear_offset[0]

    lines = lax.all_to_all(
        state.reshape(groups, planes, rows, cols), "gy", split_axis=0, concat_axis=0, tiled=True
    )
    low = passed_along(lines[:, :, rows - DEPTH :], "gx", 1)
    high = passed_along(lines[:, :, :DEPTH], "gx", -1)
    low_shift = passed_along(shift_rows[rows - DEPTH :], "gx", 1)
    high_shift = passed_along(shift_rows[:DEPTH], "gx", -1)
    shifts = jnp.concatenate(
        [
            low_shift - jnp.where(row_dev == 0, offset, 0),
            shift_rows,
            high_shift + jnp.where(row_dev == radial_count - 1, offset, 0),
        ]
    )
    shifts = (shifts + DEPTH) % cells_y
    chunk = turn_lines(groups, rows, planes)(
        shifts,
        lines.reshape(groups, planes * rows, cols),
        low.reshape(groups, planes * DEPTH, cols),
        high.reshape(groups, planes * DEPTH, cols),
    )
    wide = lax.all_to_all(
        chunk.reshape(groups, -1, cols), "gy", split_axis=0, concat_axis=0, tiled=True
    )
    padded = jnp.concatenate([residual[-DEPTH:], residual, residual[:DEPTH]])
    drift = lax.dynamic_slice_in_dim(padded, row_dev * rows, rows + 2 * DEPTH)
    evolved = two_sections(fields, depth, rows)(drift, wide.reshape(-1, cols))
    return evolved.reshape(state.shape)


def solution(mesh):
    return jax.shard_map(
        local,
        mesh=mesh,
        in_specs=(P(None, None, "gx", "gy"), P(), P("gx"), P()),
        out_specs=P(None, None, "gx", "gy"),
        check_vma=False,
    )
```

profile of v0, /device:TPU:1, one launch (start us, length us, event | category | flops | bytes accessed | tf_op | source)
XLA Modules:
  0.0 59.6 jit_solution(4961955033778878141)
XLA Ops:
  0.0 0.0 copy-start.1
  0.0 9.4 %all-to-all-start = ((f32[16,4,16,128]{3,2,1,0:T(8,128)}), f32[16,4,16,128]{3,2,1,0:T(8,128)S(1)}, u32[]{:S(2)}, u32[]{:S(2)}) async-start(f32[16,4,16,128]{3,2,1,0:T(8,128)} %bitcast.14), calls=%async_computation | async-start | bytes 1048576 | tf_op jit(solution)/shard_map/all_to_all | solution.py:318
  9.4 0.0 copy-done.1
  9.4 0.1 fusion.2
  9.5 0.8 %collective-permute-start = (s32[2]{0:T(128)S(1)}, s32[2]{0:T(128)S(1)}, u32[]{:S(2)}, u32[]{:S(2)}) collective-permute-start(s32[2]{0:T(128)S(1)} %get-tuple-element.7), channel_id=1, source_target_pairs={{0,16},{16,32},{32,48},{48,64},{64,80},{80,96},{96,112},{112,0},{1... | collective-permute-start | bytes 32 | tf_op jit(solution)/shard_map/ppermute | solution.py:23
  10.3 2.8 %collective-permute-start.1 = (s32[2]{0:T(128)S(1)}, s32[2]{0:T(128)S(1)}, u32[]{:S(2)}, u32[]{:S(2)}) collective-permute-start(s32[2]{0:T(128)S(1)} %get-tuple-element.8), channel_id=1, source_target_pairs={{0,112},{16,0},{32,16},{48,32},{64,48},{80,64},{96,80},{112,96},{1... | collective-permute-start | bytes 32 | tf_op jit(solution)/shard_map/ppermute | solution.py:23
  13.8 0.6 collective-permute-done
  14.3 0.0 collective-permute-done.1
  14.4 6.5 %all-to-all-done = f32[16,4,16,128]{3,2,1,0:T(8,128)S(1)} async-done(((f32[16,4,16,128]{3,2,1,0:T(8,128)}), f32[16,4,16,128]{3,2,1,0:T(8,128)S(1)}, u32[]{:S(2)}, u32[]{:S(2)}) %all-to-all-start) | async-done | bytes 524320 | tf_op jit(solution)/shard_map/all_to_all | solution.py:318
  20.9 3.0 %collective-permute-start.3 = (f32[16,4,2,128]{3,2,1,0:T(2,128)S(1)}, f32[16,4,2,128]{3,2,1,0:T(2,128)S(1)}, u32[]{:S(2)}, u32[]{:S(2)}) collective-permute-start(f32[16,4,2,128]{3,2,1,0:T(2,128)S(1)} %get-tuple-element.5), channel_id=1, source_target_pairs={{0,112},{16,0},{32,16},{48,32},{64,48},{80,64},{96,80},{112,96},{1... | collective-permute-start | bytes 196616 | tf_op jit(solution)/shard_map/ppermute | solution.py:23
  23.9 0.0 collective-permute-start.2
  23.9 0.1 and_select_fusion.shifts
  24.0 1.2 %collective-permute-done.3 = f32[16,4,2,128]{3,2,1,0:T(2,128)S(1)} collective-permute-done((f32[16,4,2,128]{3,2,1,0:T(2,128)S(1)}, f32[16,4,2,128]{3,2,1,0:T(2,128)S(1)}, u32[]{:S(2)}, u32[]{:S(2)}) %collective-permute-start.3) | collective-permute-done | bytes 65568 | tf_op jit(solution)/shard_map/ppermute | solution.py:23
  25.2 3.9 %collective-permute-done.2 = f32[16,4,2,128]{3,2,1,0:T(2,128)S(1)} collective-permute-done((f32[16,4,2,128]{3,2,1,0:T(2,128)S(1)}, f32[16,4,2,128]{3,2,1,0:T(2,128)S(1)}, u32[]{:S(2)}, u32[]{:S(2)}) %collective-permute-start.2) | collective-permute-done | bytes 65568 | tf_op jit(solution)/shard_map/ppermute | solution.py:23
  29.1 2.8 %turn_lines.1 = f32[1408,128]{1,0:T(8,128)} custom-call(s32[20]{0:T(128)S(1)} %and_select_fusion.shifts, f32[16,64,128]{2,1,0:T(8,128)S(1)} %bitcast.11, f32[16,8,128]{2,1,0:T(8,128)S(1)} %bitcast.13, f32[16,8,128]{2,1,0:T(8,128)S(1)} %bitcast.12), custom_call_target="tpu_custom_call" | custom-call | tf_op jit(solution)/shard_map/turn_lines/pallas_call | solution.py:333
  31.9 5.9 %all-to-all-start.1 = ((f32[16,88,128]{2,1,0:T(8,128)}), f32[16,88,128]{2,1,0:T(8,128)S(1)}, u32[]{:S(2)}, u32[]{:S(2)}) async-start(f32[16,88,128]{2,1,0:T(8,128)} %bitcast.5), calls=%async_computation.1 | async-start | bytes 1441792 | tf_op jit(solution)/shard_map/all_to_all | solution.py:339
  37.8 0.0 copy-start
  37.8 0.6 %copy-done = f32[128]{0:T(128)S(1)} copy-done((f32[128]{0:T(128)S(1)}, f32[128]{0:T(128)}, u32[]{:S(2)}) %copy-start) | copy-done | bytes 536
  38.4 0.1 fusion.3
  38.5 0.1 pad_maximum_fusion
  38.6 0.1 dynamic_slice.3.residual
  38.7 13.0 %all-to-all-done.1 = f32[16,88,128]{2,1,0:T(8,128)S(1)} async-done(((f32[16,88,128]{2,1,0:T(8,128)}), f32[16,88,128]{2,1,0:T(8,128)S(1)}, u32[]{:S(2)}, u32[]{:S(2)}) %all-to-all-start.1) | async-done | bytes 720928 | tf_op jit(solution)/shard_map/all_to_all | solution.py:339
  51.6 8.0 %two_sections.1 = f32[1024,128]{1,0:T(8,128)} custom-call(f32[20]{0:T(128)S(1)} %dynamic_slice.3.residual, f32[1408,128]{1,0:T(8,128)S(1)} %bitcast.10), custom_call_target="tpu_custom_call" | custom-call | tf_op jit(solution)/shard_map/two_sections/pallas_call | solution.py:344
  (3 shorter events, 0.1 us)
Async XLA Ops:
  0.0 9.4 %copy-start.1 = (s32[16]{0:T(128)S(1)}, s32[16]{0:T(128)}, u32[]{:S(2)}) copy-start(s32[16]{0:T(128)} %param.6) | copy-start | bytes 196
  0.0 20.8 %all-to-all-start = ((f32[16,4,16,128]{3,2,1,0:T(8,128)}), f32[16,4,16,128]{3,2,1,0:T(8,128)S(1)}, u32[]{:S(2)}, u32[]{:S(2)}) async-start(f32[16,4,16,128]{3,2,1,0:T(8,128)} %bitcast.14), calls=%async_computation | async-start | bytes 1048576 | tf_op jit(solution)/shard_map/all_to_all | solution.py:318
  9.5 4.8 %collective-permute-start = (s32[2]{0:T(128)S(1)}, s32[2]{0:T(128)S(1)}, u32[]{:S(2)}, u32[]{:S(2)}) collective-permute-start(s32[2]{0:T(128)S(1)} %get-tuple-element.7), channel_id=1, source_target_pairs={{0,16},{16,32},{32,48},{48,64},{64,80},{80,96},{96,112},{112,0},{1... | collective-permute-start | bytes 32 | tf_op jit(solution)/shard_map/ppermute | solution.py:23
  10.3 4.1 %collective-permute-start.1 = (s32[2]{0:T(128)S(1)}, s32[2]{0:T(128)S(1)}, u32[]{:S(2)}, u32[]{:S(2)}) collective-permute-start(s32[2]{0:T(128)S(1)} %get-tuple-element.8), channel_id=1, source_target_pairs={{0,112},{16,0},{32,16},{48,32},{64,48},{80,64},{96,80},{112,96},{1... | collective-permute-start | bytes 32 | tf_op jit(solution)/shard_map/ppermute | solution.py:23
  20.9 4.3 %collective-permute-start.3 = (f32[16,4,2,128]{3,2,1,0:T(2,128)S(1)}, f32[16,4,2,128]{3,2,1,0:T(2,128)S(1)}, u32[]{:S(2)}, u32[]{:S(2)}) collective-permute-start(f32[16,4,2,128]{3,2,1,0:T(2,128)S(1)} %get-tuple-element.5), channel_id=1, source_target_pairs={{0,112},{16,0},{32,16},{48,32},{64,48},{80,64},{96,80},{112,96},{1... | collective-permute-start | bytes 196616 | tf_op jit(solution)/shard_map/ppermute | solution.py:23
  23.9 5.2 %collective-permute-start.2 = (f32[16,4,2,128]{3,2,1,0:T(2,128)S(1)}, f32[16,4,2,128]{3,2,1,0:T(2,128)S(1)}, u32[]{:S(2)}, u32[]{:S(2)}) collective-permute-start(f32[16,4,2,128]{3,2,1,0:T(2,128)S(1)} %get-tuple-element.6), channel_id=1, source_target_pairs={{0,16},{16,32},{32,48},{48,64},{64,80},{80,96},{96,112},{112,0},{1... | collective-permute-start | bytes 196616 | tf_op jit(solution)/shard_map/ppermute | solution.py:23
  31.9 19.7 %all-to-all-start.1 = ((f32[16,88,128]{2,1,0:T(8,128)}), f32[16,88,128]{2,1,0:T(8,128)S(1)}, u32[]{:S(2)}, u32[]{:S(2)}) async-start(f32[16,88,128]{2,1,0:T(8,128)} %bitcast.5), calls=%async_computation.1 | async-start | bytes 1441792 | tf_op jit(solution)/shard_map/all_to_all | solution.py:339
  37.8 0.7 %copy-start = (f32[128]{0:T(128)S(1)}, f32[128]{0:T(128)}, u32[]{:S(2)}) copy-start(f32[128]{0:T(128)} %param.5) | copy-start | bytes 1540
where the time goes:
time: 60 us; the launch traced here: 59.6 us
  waiting for transfers between devices  25.1 us (42%)
  starting transfers between devices  22 us (37%)
  Pallas kernels  10.8 us (18%)
  local copies, waits for them, and re-layouts  0.92 us (2%)
  between operations  0.69 us (1%)
    all_to_all x1, waiting for transfers between devices, local(): lax.all_to_all(chunk.reshape(groups, -1, cols), 'gy', split_axis=0, conca...  13 us
    all_to_all x1, starting transfers between devices, local(): lax.all_to_all(state.reshape(groups, planes, rows, cols), 'gy', split_axi...  9.43 us
    pallas_call x1, Pallas kernels, local(): evolved = two_sections(fields, depth, rows)(drift, wide.reshape(-1, cols))  8.03 us
    ppermute x4, starting transfers between devices, passed_along(): return lax.ppermute(value, axis, pairs)  6.61 us
    all_to_all x1, waiting for transfers between devices, local(): lax.all_to_all(state.reshape(groups, planes, rows, cols), 'gy', split_axi...  6.47 us
    all_to_all x1, starting transfers between devices, local(): lax.all_to_all(chunk.reshape(groups, -1, cols), 'gy', split_axis=0, conca...  5.91 us
    ppermute x4, waiting for transfers between devices, passed_along(): return lax.ppermute(value, axis, pairs)  5.7 us
    pallas_call x1, Pallas kernels, local(): turn_lines(groups, rows, planes)  2.75 us
  transfers between devices with their start and end apart: 6, of which 5 were waited for; matrix products, arithmetic and copies ran while one was open for 1% of the time, Pallas kernels for 0%

commit v1 on v0

--- a/solution.py
+++ b/solution.py
@@ -268,7 +268,7 @@
         for row in (strip_at + 1, strip_at + 2):
             edges = first_row(row, edges)
         widen_strips(first)
-        lax.fori_loop(1, wide - 1, first_row, edges_of(moved, 1))
+        lax.fori_loop(1, wide - 1, first_row, edges_of(moved, 1), unroll=3)
 
         edges = edges_of(first, strip_at + 1)
         for parity in range(2):
@@ -288,7 +288,7 @@
                 )
             return edges
 
-        lax.fori_loop(DEPTH, wide - DEPTH, second_row, edges_of(first, DEPTH))
+        lax.fori_loop(DEPTH, wide - DEPTH, second_row, edges_of(first, DEPTH), unroll=4)
 
     return pl.pallas_call(
         kernel,

time: 60 us -> 56.2 us (0.937)
  Pallas kernels: 10.8 us -> 7.03 us
    pallas_call x1, Pallas kernels: 8.03 us -> 4.28 us  [local(): evolved = two_sections(fields, depth, rows)(drift, wide.reshape(-1, cols))]
where the time goes in v1:
time: 56.2 us; the launch traced here: 55.9 us
  waiting for transfers between devices  25.1 us (45%)
  starting transfers between devices  22 us (39%)
  Pallas kernels  7.03 us (13%)
  local copies, waits for them, and re-layouts  0.92 us (2%)
  between operations  0.69 us (1%)
    all_to_all x1, waiting for transfers between devices, local(): lax.all_to_all(chunk.reshape(groups, -1, cols), 'gy', split_axis=0, conca...  13 us
    all_to_all x1, starting transfers between devices, local(): lax.all_to_all(state.reshape(groups, planes, rows, cols), 'gy', split_axi...  9.43 us
    ppermute x4, starting transfers between devices, passed_along(): return lax.ppermute(value, axis, pairs)  6.61 us
    all_to_all x1, waiting for transfers between devices, local(): lax.all_to_all(state.reshape(groups, planes, rows, cols), 'gy', split_axi...  6.47 us
    all_to_all x1, starting transfers between devices, local(): lax.all_to_all(chunk.reshape(groups, -1, cols), 'gy', split_axis=0, conca...  5.91 us
    ppermute x4, waiting for transfers between devices, passed_along(): return lax.ppermute(value, axis, pairs)  5.7 us
    pallas_call x1, Pallas kernels, local(): evolved = two_sections(fields, depth, rows)(drift, wide.reshape(-1, cols))  4.28 us
    pallas_call x1, Pallas kernels, local(): turn_lines(groups, rows, planes)  2.75 us
  transfers between devices with their start and end apart: 6, of which 5 were waited for; matrix products, arithmetic and copies ran while one was open for 1% of the time, Pallas kernels for 0%

profile of v1, /device:TPU:1, one launch (start us, length us, event | category | flops | bytes accessed | tf_op | source)
XLA Modules:
  0.0 55.9 jit_solution(7399181416364399435)
XLA Ops:
  0.0 0.0 copy-start.1
  0.0 9.4 %all-to-all-start = ((f32[16,4,16,128]{3,2,1,0:T(8,128)}), f32[16,4,16,128]{3,2,1,0:T(8,128)S(1)}, u32[]{:S(2)}, u32[]{:S(2)}) async-start(f32[16,4,16,128]{3,2,1,0:T(8,128)} %bitcast.14), calls=%async_computation | async-start | bytes 1048576 | tf_op jit(solution)/shard_map/all_to_all | solution.py:318
  9.4 0.0 copy-done.1
  9.4 0.1 fusion.2
  9.5 0.8 %collective-permute-start = (s32[2]{0:T(128)S(1)}, s32[2]{0:T(128)S(1)}, u32[]{:S(2)}, u32[]{:S(2)}) collective-permute-start(s32[2]{0:T(128)S(1)} %get-tuple-element.7), channel_id=1, source_target_pairs={{0,16},{16,32},{32,48},{48,64},{64,80},{80,96},{96,112},{112,0},{1... | collective-permute-start | bytes 32 | tf_op jit(solution)/shard_map/ppermute | solution.py:23
  10.3 2.8 %collective-permute-start.1 = (s32[2]{0:T(128)S(1)}, s32[2]{0:T(128)S(1)}, u32[]{:S(2)}, u32[]{:S(2)}) collective-permute-start(s32[2]{0:T(128)S(1)} %get-tuple-element.8), channel_id=1, source_target_pairs={{0,112},{16,0},{32,16},{48,32},{64,48},{80,64},{96,80},{112,96},{1... | collective-permute-start | bytes 32 | tf_op jit(solution)/shard_map/ppermute | solution.py:23
  13.8 0.6 %collective-permute-done = s32[2]{0:T(128)S(1)} collective-permute-done((s32[2]{0:T(128)S(1)}, s32[2]{0:T(128)S(1)}, u32[]{:S(2)}, u32[]{:S(2)}) %collective-permute-start) | collective-permute-done | bytes 40 | tf_op jit(solution)/shard_map/ppermute | solution.py:23
  14.3 0.0 collective-permute-done.1
  14.4 6.5 %all-to-all-done = f32[16,4,16,128]{3,2,1,0:T(8,128)S(1)} async-done(((f32[16,4,16,128]{3,2,1,0:T(8,128)}), f32[16,4,16,128]{3,2,1,0:T(8,128)S(1)}, u32[]{:S(2)}, u32[]{:S(2)}) %all-to-all-start) | async-done | bytes 524320 | tf_op jit(solution)/shard_map/all_to_all | solution.py:318
  20.9 3.0 %collective-permute-start.3 = (f32[16,4,2,128]{3,2,1,0:T(2,128)S(1)}, f32[16,4,2,128]{3,2,1,0:T(2,128)S(1)}, u32[]{:S(2)}, u32[]{:S(2)}) collective-permute-start(f32[16,4,2,128]{3,2,1,0:T(2,128)S(1)} %get-tuple-element.5), channel_id=1, source_target_pairs={{0,112},{16,0},{32,16},{48,32},{64,48},{80,64},{96,80},{112,96},{1... | collective-permute-start | bytes 196616 | tf_op jit(solution)/shard_map/ppermute | solution.py:23
  23.9 0.0 collective-permute-start.2
  23.9 0.1 and_select_fusion.shifts
  24.0 1.2 %collective-permute-done.3 = f32[16,4,2,128]{3,2,1,0:T(2,128)S(1)} collective-permute-done((f32[16,4,2,128]{3,2,1,0:T(2,128)S(1)}, f32[16,4,2,128]{3,2,1,0:T(2,128)S(1)}, u32[]{:S(2)}, u32[]{:S(2)}) %collective-permute-start.3) | collective-permute-done | bytes 65568 | tf_op jit(solution)/shard_map/ppermute | solution.py:23
  25.2 3.9 %collective-permute-done.2 = f32[16,4,2,128]{3,2,1,0:T(2,128)S(1)} collective-permute-done((f32[16,4,2,128]{3,2,1,0:T(2,128)S(1)}, f32[16,4,2,128]{3,2,1,0:T(2,128)S(1)}, u32[]{:S(2)}, u32[]{:S(2)}) %collective-permute-start.2) | collective-permute-done | bytes 65568 | tf_op jit(solution)/shard_map/ppermute | solution.py:23
  29.1 2.8 %turn_lines.1 = f32[1408,128]{1,0:T(8,128)} custom-call(s32[20]{0:T(128)S(1)} %and_select_fusion.shifts, f32[16,64,128]{2,1,0:T(8,128)S(1)} %bitcast.11, f32[16,8,128]{2,1,0:T(8,128)S(1)} %bitcast.13, f32[16,8,128]{2,1,0:T(8,128)S(1)} %bitcast.12), custom_call_target="tpu_custom_call" | custom-call | tf_op jit(solution)/shard_map/turn_lines/pallas_call | solution.py:333
  31.9 5.9 %all-to-all-start.1 = ((f32[16,88,128]{2,1,0:T(8,128)}), f32[16,88,128]{2,1,0:T(8,128)S(1)}, u32[]{:S(2)}, u32[]{:S(2)}) async-start(f32[16,88,128]{2,1,0:T(8,128)} %bitcast.5), calls=%async_computation.1 | async-start | bytes 1441792 | tf_op jit(solution)/shard_map/all_to_all | solution.py:339
  37.8 0.0 copy-start
  37.8 0.6 %copy-done = f32[128]{0:T(128)S(1)} copy-done((f32[128]{0:T(128)S(1)}, f32[128]{0:T(128)}, u32[]{:S(2)}) %copy-start) | copy-done | bytes 536
  38.4 0.1 fusion.3
  38.5 0.1 pad_maximum_fusion
  38.6 0.1 dynamic_slice.3.residual
  38.7 13.0 %all-to-all-done.1 = f32[16,88,128]{2,1,0:T(8,128)S(1)} async-done(((f32[16,88,128]{2,1,0:T(8,128)}), f32[16,88,128]{2,1,0:T(8,128)S(1)}, u32[]{:S(2)}, u32[]{:S(2)}) %all-to-all-start.1) | async-done | bytes 720928 | tf_op jit(solution)/shard_map/all_to_all | solution.py:339
  51.6 4.3 %two_sections.1 = f32[1024,128]{1,0:T(8,128)} custom-call(f32[20]{0:T(128)S(1)} %dynamic_slice.3.residual, f32[1408,128]{1,0:T(8,128)S(1)} %bitcast.10), custom_call_target="tpu_custom_call" | custom-call | tf_op jit(solution)/shard_map/two_sections/pallas_call | solution.py:344
  (3 shorter events, 0.1 us)
Async XLA Ops:
  0.0 9.4 %copy-start.1 = (s32[16]{0:T(128)S(1)}, s32[16]{0:T(128)}, u32[]{:S(2)}) copy-start(s32[16]{0:T(128)} %param.6) | copy-start | bytes 196
  0.0 20.8 %all-to-all-start = ((f32[16,4,16,128]{3,2,1,0:T(8,128)}), f32[16,4,16,128]{3,2,1,0:T(8,128)S(1)}, u32[]{:S(2)}, u32[]{:S(2)}) async-start(f32[16,4,16,128]{3,2,1,0:T(8,128)} %bitcast.14), calls=%async_computation | async-start | bytes 1048576 | tf_op jit(solution)/shard_map/all_to_all | solution.py:318
  9.5 4.8 %collective-permute-start = (s32[2]{0:T(128)S(1)}, s32[2]{0:T(128)S(1)}, u32[]{:S(2)}, u32[]{:S(2)}) collective-permute-start(s32[2]{0:T(128)S(1)} %get-tuple-element.7), channel_id=1, source_target_pairs={{0,16},{16,32},{32,48},{48,64},{64,80},{80,96},{96,112},{112,0},{1... | collective-permute-start | bytes 32 | tf_op jit(solution)/shard_map/ppermute | solution.py:23
  10.3 4.1 %collective-permute-start.1 = (s32[2]{0:T(128)S(1)}, s32[2]{0:T(128)S(1)}, u32[]{:S(2)}, u32[]{:S(2)}) collective-permute-start(s32[2]{0:T(128)S(1)} %get-tuple-element.8), channel_id=1, source_target_pairs={{0,112},{16,0},{32,16},{48,32},{64,48},{80,64},{96,80},{112,96},{1... | collective-permute-start | bytes 32 | tf_op jit(solution)/shard_map/ppermute | solution.py:23
  20.9 4.3 %collective-permute-start.3 = (f32[16,4,2,128]{3,2,1,0:T(2,128)S(1)}, f32[16,4,2,128]{3,2,1,0:T(2,128)S(1)}, u32[]{:S(2)}, u32[]{:S(2)}) collective-permute-start(f32[16,4,2,128]{3,2,1,0:T(2,128)S(1)} %get-tuple-element.5), channel_id=1, source_target_pairs={{0,112},{16,0},{32,16},{48,32},{64,48},{80,64},{96,80},{112,96},{1... | collective-permute-start | bytes 196616 | tf_op jit(solution)/shard_map/ppermute | solution.py:23
  23.9 5.2 %collective-permute-start.2 = (f32[16,4,2,128]{3,2,1,0:T(2,128)S(1)}, f32[16,4,2,128]{3,2,1,0:T(2,128)S(1)}, u32[]{:S(2)}, u32[]{:S(2)}) collective-permute-start(f32[16,4,2,128]{3,2,1,0:T(2,128)S(1)} %get-tuple-element.6), channel_id=1, source_target_pairs={{0,16},{16,32},{32,48},{48,64},{64,80},{80,96},{96,112},{112,0},{1... | collective-permute-start | bytes 196616 | tf_op jit(solution)/shard_map/ppermute | solution.py:23
  31.9 19.7 %all-to-all-start.1 = ((f32[16,88,128]{2,1,0:T(8,128)}), f32[16,88,128]{2,1,0:T(8,128)S(1)}, u32[]{:S(2)}, u32[]{:S(2)}) async-start(f32[16,88,128]{2,1,0:T(8,128)} %bitcast.5), calls=%async_computation.1 | async-start | bytes 1441792 | tf_op jit(solution)/shard_map/all_to_all | solution.py:339
  37.8 0.7 %copy-start = (f32[128]{0:T(128)S(1)}, f32[128]{0:T(128)}, u32[]{:S(2)}) copy-start(f32[128]{0:T(128)} %param.5) | copy-start | bytes 1540

commit v2 on v1

--- a/solution.py
+++ b/solution.py
@@ -13,6 +13,7 @@
 shear_rate = 1.5
 
 LANES = 128
+TILE_ROWS = 8
 DEPTH = 2
 STRIP = 4 * DEPTH
 
@@ -23,80 +24,140 @@
     return lax.ppermute(value, axis, pairs)
 
 
-def turn_lines(groups, rows, planes):
+def turned_line(flat, first_row, total, groups, amount, lane):
+    block = (groups - amount // LANES) % groups
+    part = amount % LANES
+    keep = lane < LANES - part
+    edge = ((lane + part) & (LANES - 1)) < 2 * DEPTH
+    before, here, after = (
+        flat[pl.ds((block + ahead_by) * total + first_row, groups, stride=total), :]
+        for ahead_by in range(3)
+    )
+    window = jnp.where(keep, here, before)
+    rim = jnp.where(edge, jnp.where(keep, after, here), window)
+    return pltpu.roll(window, part, 1), rim, part
+
+
+def placed_strip(rim, part, place, lane, strips):
+    turn = (part + 2 * DEPTH + STRIP * place) % LANES
+    in_place = (lane >= STRIP * place) & (lane < STRIP * (place + 1))
+    return jnp.where(in_place, pltpu.roll(rim, turn, 1), strips)
+
+
+def lay_twice(source, lines, start, size, groups):
+    for block in range(groups):
+        value = source[block]
+        for target in (block + 1, block + 1 + groups):
+            lines[target, pl.ds(start, size)] = value
+        if block == groups - 1:
+            lines[0, pl.ds(start, size)] = value
+
+
+def turn_own(groups, rows, planes):
+    own = rows * planes
+    zone = planes * (2 * DEPTH + 2)
+
+    def kernel(shifts, mine, out, strips_out, lines, windows, out_sem):
+        lay_twice(mine, lines, 0, own, groups)
+        flat = lines.reshape((2 * groups + 1) * own, LANES)
+        target = windows.reshape(groups * own, LANES)
+        lane = lax.broadcasted_iota(jnp.int32, (groups, LANES), 1)
+        strips = [[jnp.zeros((groups, LANES), jnp.float32) for _ in range(planes)] for _ in range(2)]
+        for row in range(rows):
+            wide_row = row + DEPTH
+            for plane in range(planes):
+                line = plane * rows + row
+                window, rim, part = turned_line(flat, line, own, groups, shifts[wide_row], lane)
+                target[pl.ds(line, groups, stride=own), :] = window
+                strips[wide_row % 2][plane] = placed_strip(
+                    rim, part, wide_row // 2, lane, strips[wide_row % 2][plane]
+                )
+        for plane in range(planes):
+            for parity in range(2):
+                strips_out[plane * 2 + parity] = strips[parity][plane]
+        leave = pltpu.make_async_copy(windows, out.at[:, pl.ds(0, own)], out_sem)
+        leave.start()
+        leave.wait()
+
+    return pl.pallas_call(
+        kernel,
+        in_specs=[pl.BlockSpec(memory_space=pltpu.SMEM), pl.BlockSpec(memory_space=pltpu.VMEM)],
+        out_shape=(
+            jax.ShapeDtypeStruct((groups, own + zone, LANES), jnp.float32),
+            jax.ShapeDtypeStruct((2 * planes, groups, LANES), jnp.float32),
+        ),
+        out_specs=(pl.BlockSpec(memory_space=pl.ANY), pl.BlockSpec(memory_space=pltpu.VMEM)),
+        scratch_shapes=[
+            pltpu.VMEM((2 * groups + 1, own, LANES), jnp.float32),
+            pltpu.VMEM((groups, own, LANES), jnp.float32),
+            pltpu.SemaphoreType.DMA,
+        ],
+        compiler_params=pltpu.CompilerParams(vmem_limit_bytes=24 * 1024 * 1024),
+        cost_estimate=pl.CostEstimate(flops=4000000, bytes_accessed=4000000, transcendentals=0),
+        name="turn_own",
+    )
+
+
+def turn_ghost(groups, rows, planes):
     own = rows * planes
     ghost = DEPTH * planes
-    total = own + 2 * ghost
-    wide = rows + 2 * DEPTH
-    pitch = wide + 2
-
-    def kernel(shifts, mine, low, high, out, lines, sems):
+    zone = 3 * ghost
+
+    def kernel(shifts, low, high, strips_in, chunk, out, lines, windows, sems):
+        lay_twice(low, lines, 0, ghost, groups)
+        lay_twice(high, lines, ghost, ghost, groups)
+        flat = lines.reshape((2 * groups + 1) * 2 * ghost, LANES)
+        target = windows.reshape(3 * groups * ghost, LANES)
+        lane = lax.broadcasted_iota(jnp.int32, (groups, LANES), 1)
+        strips = [
+            [strips_in[plane * 2 + parity] for plane in range(planes)] for parity in range(2)
+        ]
+
+        def leave(part):
+            copy = pltpu.make_async_copy(
+                windows.at[part], out.at[:, pl.ds(own + part * ghost, ghost)], sems.at[part]
+            )
+            copy.start()
+            return copy
+
         copies = []
-        for part, (source, start, size) in enumerate(
-            ((mine, 0, own), (low, own, ghost), (high, own + ghost, ghost))
-        ):
-            for turn, (first, count, target) in enumerate(
-                ((0, groups, 1), (0, groups, groups + 1), (groups - 1, 1, 0))
-            ):
-                copies.append(
-                    pltpu.make_async_copy(
-                        source.at[pl.ds(first, count)],
-                        lines.at[pl.ds(target, count), pl.ds(start, size)],
-                        sems.at[part, turn],
+        for side in range(2):
+            for row in range(DEPTH):
+                wide_row = row + side * (rows + DEPTH)
+                for plane in range(planes):
+                    line = side * ghost + plane * DEPTH + row
+                    window, rim, part = turned_line(
+                        flat, line, 2 * ghost, groups, shifts[wide_row], lane
                     )
-                )
-        for copy in copies:
-            copy.start()
+                    place = side * groups * ghost + plane * DEPTH + row
+                    target[pl.ds(place, groups, stride=ghost), :] = window
+                    strips[wide_row % 2][plane] = placed_strip(
+                        rim, part, wide_row // 2, lane, strips[wide_row % 2][plane]
+                    )
+            copies.append(leave(side))
+        for plane in range(planes):
+            for parity in range(2):
+                place = 2 * groups * ghost + plane * DEPTH + parity
+                target[pl.ds(place, groups, stride=ghost), :] = strips[parity][plane]
+        copies.append(leave(2))
         for copy in copies:
             copy.wait()
-        flat = lines.reshape((2 * groups + 1) * total, LANES)
-        lane = lax.broadcasted_iota(jnp.int32, (groups, LANES), 1)
-        strips = [[jnp.zeros((groups, LANES), jnp.float32) for _ in range(planes)] for _ in range(2)]
-        for row in range(wide):
-            amount = shifts[row]
-            block = (groups - amount // LANES) % groups
-            part = amount % LANES
-            keep = lane < LANES - part
-            edge = ((lane + part) & (LANES - 1)) < 2 * DEPTH
-            place = row // 2
-            strip_turn = (part + 2 * DEPTH + STRIP * place) % LANES
-            in_place = (lane >= STRIP * place) & (lane < STRIP * (place + 1))
-            for plane in range(planes):
-                if row < DEPTH:
-                    line = own + plane * DEPTH + row
-                elif row < DEPTH + rows:
-                    line = plane * rows + row - DEPTH
-                else:
-                    line = own + ghost + plane * DEPTH + row - DEPTH - rows
-                before, here, after = (
-                    flat[pl.ds((block + ahead_by) * total + line, groups, stride=total), :]
-                    for ahead_by in range(3)
-                )
-                window = jnp.where(keep, here, before)
-                out[pl.ds(plane * pitch + row, groups, stride=planes * pitch), :] = pltpu.roll(
-                    window, part, 1
-                )
-                rim = jnp.where(edge, jnp.where(keep, after, here), window)
-                strips[row % 2][plane] = jnp.where(
-                    in_place, pltpu.roll(rim, strip_turn, 1), strips[row % 2][plane]
-                )
-        for parity in range(2):
-            for plane in range(planes):
-                out[pl.ds(plane * pitch + wide + parity, groups, stride=planes * pitch), :] = strips[
-                    parity
-                ][plane]
 
     return pl.pallas_call(
         kernel,
-        in_specs=[pl.BlockSpec(memory_space=pltpu.SMEM)] + [pl.BlockSpec(memory_space=pl.ANY)] * 3,
-        out_shape=jax.ShapeDtypeStruct((groups * planes * pitch, LANES), jnp.float32),
-        out_specs=pl.BlockSpec(memory_space=pltpu.VMEM),
+        in_specs=[pl.BlockSpec(memory_space=pltpu.SMEM)]
+        + [pl.BlockSpec(memory_space=pltpu.VMEM)] * 3
+        + [pl.BlockSpec(memory_space=pl.ANY)],
+        out_shape=jax.ShapeDtypeStruct((groups, own + zone, LANES), jnp.float32),
+        out_specs=pl.BlockSpec(memory_space=pl.ANY),
+        input_output_aliases={4: 0},
         scratch_shapes=[
-            pltpu.VMEM((2 * groups + 1, total, LANES), jnp.float32),
-            pltpu.SemaphoreType.DMA((3, 3)),
+            pltpu.VMEM((2 * groups + 1, 2 * ghost, LANES), jnp.float32),
+            pltpu.VMEM((3, groups, ghost, LANES), jnp.float32),
+            pltpu.SemaphoreType.DMA((3,)),
         ],
         compiler_params=pltpu.CompilerParams(vmem_limit_bytes=24 * 1024 * 1024),
-        name="turn_lines",
+        name="turn_ghost",
     )
 
 
@@ -212,10 +273,14 @@
 
 def two_sections(fields, depth, rows):
     wide = rows + 2 * DEPTH
-    pitch = wide + 2
+    half = depth // 2
+    own = half * rows
+    ghost = half * DEPTH
+    chunk = own + 3 * ghost
     strip_at = wide
 
-    def kernel(residual, source, out, moved, first, drift_rows, ends):
+    def kernel(residual, source, out, moved, first, drift_rows, ends, evolved, sems):
+        flat_out = evolved.reshape(fields * depth * rows, LANES)
         lane = lax.broadcasted_iota(jnp.int32, (depth, LANES), 1)
 
         def widen_strips(ref):
@@ -234,11 +299,24 @@
         drift_rows[strip_at + 1] = strip_drift[0]
         drift_rows[strip_at + 2] = strip_drift[1]
         drift_rows[strip_at + 3] = pltpu.roll(strip_drift[0], LANES - STRIP, 1)
+        under = lax.broadcasted_iota(jnp.int32, (depth, LANES), 0) < half
+
+        def column(first, stride):
+            return jnp.where(
+                under,
+                source[pl.ds(first, depth, stride=stride), :],
+                source[pl.ds(first + chunk - half * stride, depth, stride=stride), :],
+            )
+
         for field in range(fields):
-            for row in range(pitch):
-                moved[field, row if row < wide else row + 1] = source[
-                    pl.ds(field * depth * pitch + row, depth, stride=pitch), :
-                ]
+            start = 2 * field * chunk
+            for row in range(rows):
+                moved[field, row + DEPTH] = column(start + row, rows)
+            for entry in range(DEPTH):
+                first_at = start + own + entry
+                moved[field, entry] = column(first_at, DEPTH)
+                moved[field, DEPTH + rows + entry] = column(first_at + ghost, DEPTH)
+                moved[field, strip_at + 1 + entry] = column(first_at + 2 * ghost, DEPTH)
         widen_strips(moved)
 
         def row_of(ref, row):
@@ -283,23 +361,36 @@
             for field in range(fields):
                 whole = 0.5 * (moved[field, row] + result[field])
                 end = pltpu.roll(ends[field, row % 2], turn, 1)
-                out[pl.ds(field * depth * rows + row - DEPTH, depth, stride=rows), :] = jnp.where(
+                flat_out[pl.ds(field * depth * rows + row - DEPTH, depth, stride=rows), :] = jnp.where(
                     lane < LANES - 2 * DEPTH, pltpu.roll(whole, LANES - DEPTH, 1), end
                 )
             return edges
 
-        lax.fori_loop(DEPTH, wide - DEPTH, second_row, edges_of(first, DEPTH), unroll=4)
+        edges = edges_of(first, DEPTH)
+        copies = []
+        for block in range(rows // TILE_ROWS):
+            start = DEPTH + block * TILE_ROWS
+            edges = lax.fori_loop(start, start + TILE_ROWS, second_row, edges, unroll=4)
+            for field in range(fields):
+                piece = (pl.ds(field * depth, depth), pl.ds(block * TILE_ROWS, TILE_ROWS))
+                copy = pltpu.make_async_copy(evolved.at[piece], out.at[piece], sems.at[block, field])
+                copy.start()
+                copies.append(copy)
+        for copy in copies:
+            copy.wait()
 
     return pl.pallas_call(
         kernel,
         in_specs=[pl.BlockSpec(memory_space=pltpu.SMEM), pl.BlockSpec(memory_space=pltpu.VMEM)],
-        out_shape=jax.ShapeDtypeStruct((fields * depth * rows, LANES), jnp.float32),
-        out_specs=pl.BlockSpec(memory_space=pltpu.VMEM),
+        out_shape=jax.ShapeDtypeStruct((fields * depth, rows, LANES), jnp.float32),
+        out_specs=pl.BlockSpec(memory_space=pl.ANY),
         scratch_shapes=[
             pltpu.VMEM((fields, wide + 4, depth, LANES), jnp.float32),
             pltpu.VMEM((fields, wide + 4, depth, LANES), jnp.float32),
             pltpu.VMEM((wide + 4, depth, LANES), jnp.float32),
             pltpu.VMEM((fields, 2, depth, LANES), jnp.float32),
+            pltpu.VMEM((fields * depth, rows, LANES), jnp.float32),
+            pltpu.SemaphoreType.DMA((rows // TILE_ROWS, fields)),
         ],
         compiler_params=pltpu.CompilerParams(vmem_limit_bytes=24 * 1024 * 1024),
         name="two_sections",
@@ -330,15 +421,18 @@
         ]
     )
     shifts = (shifts + DEPTH) % cells_y
-    chunk = turn_lines(groups, rows, planes)(
+    own_shifts = jnp.concatenate([shift_rows[:DEPTH], shift_rows]) + DEPTH
+    chunk, strips = turn_own(groups, rows, planes)(
+        own_shifts % cells_y, lines.reshape(groups, planes * rows, cols)
+    )
+    chunk = turn_ghost(groups, rows, planes)(
         shifts,
-        lines.reshape(groups, planes * rows, cols),
         low.reshape(groups, planes * DEPTH, cols),
         high.reshape(groups, planes * DEPTH, cols),
-    )
-    wide = lax.all_to_all(
-        chunk.reshape(groups, -1, cols), "gy", split_axis=0, concat_axis=0, tiled=True
-    )
+        strips,
+        chunk,
+    )
+    wide = lax.all_to_all(chunk, "gy", split_axis=0, concat_axis=0, tiled=True)
     padded = jnp.concatenate([residual[-DEPTH:], residual, residual[:DEPTH]])
     drift = lax.dynamic_slice_in_dim(padded, row_dev * rows, rows + 2 * DEPTH)
     evolved = two_sections(fields, depth, rows)(drift, wide.reshape(-1, cols))

time: 56.2 us -> 55.2 us (0.982)
  waiting for transfers between devices: 25.1 us -> 22 us
  Pallas kernels: 7.03 us -> 8.98 us
    ppermute x4, waiting for transfers between devices: 5.7 us -> 2.61 us  [passed_along(): return lax.ppermute(value, axis, pairs)]
    pallas_call x1 -> x2, Pallas kernels: 2.75 us -> 4.43 us  [the longest x1 2.99 us: local(): turn_own(groups, rows, planes)]
  transfers between devices with their start and end apart: 6 -> 6, of which waited for: 5 -> 4; matrix products, arithmetic and copies ran while one was open for 1% -> 1% of each run, Pallas kernels for 0% -> 5%
where the time goes in v2:
time: 55.2 us; the launch traced here: 54.9 us
  starting transfers between devices  22 us (40%)
  waiting for transfers between devices  22 us (40%)
  Pallas kernels  8.98 us (16%)
  local copies, waits for them, and re-layouts  0.92 us (2%)
  between operations  0.71 us (1%)
    all_to_all x1, waiting for transfers between devices, local(): wide = lax.all_to_all(chunk, 'gy', split_axis=0, concat_axis=0, tiled=True)  13 us
    all_to_all x1, starting transfers between devices, local(): lax.all_to_all(state.reshape(groups, planes, rows, cols), 'gy', split_axi...  9.43 us
    ppermute x4, starting transfers between devices, passed_along(): return lax.ppermute(value, axis, pairs)  6.61 us
    all_to_all x1, waiting for transfers between devices, local(): lax.all_to_all(state.reshape(groups, planes, rows, cols), 'gy', split_axi...  6.47 us
    all_to_all x1, starting transfers between devices, local(): wide = lax.all_to_all(chunk, 'gy', split_axis=0, concat_axis=0, tiled=True)  5.91 us
    pallas_call x1, Pallas kernels, local(): evolved = two_sections(fields, depth, rows)(drift, wide.reshape(-1, cols))  4.55 us
    pallas_call x1, Pallas kernels, local(): turn_own(groups, rows, planes)  2.99 us
    ppermute x4, waiting for transfers between devices, passed_along(): return lax.ppermute(value, axis, pairs)  2.61 us
  transfers between devices with their start and end apart: 6, of which 4 were waited for; matrix products, arithmetic and copies ran while one was open for 1% of the time, Pallas kernels for 5%

profile of v2, /device:TPU:1, one launch (start us, length us, event | category | flops | bytes accessed | tf_op | source)
XLA Modules:
  0.0 54.9 jit_solution(18289219813521255041)
XLA Ops:
  0.0 0.0 copy-start.1
  0.0 9.4 %all-to-all-start = ((f32[16,4,16,128]{3,2,1,0:T(8,128)}), f32[16,4,16,128]{3,2,1,0:T(8,128)S(1)}, u32[]{:S(2)}, u32[]{:S(2)}) async-start(f32[16,4,16,128]{3,2,1,0:T(8,128)} %bitcast.13), calls=%async_computation | async-start | bytes 1048576 | tf_op jit(solution)/shard_map/all_to_all | solution.py:409
  9.4 0.0 copy-done.1
  9.4 0.1 fusion.3
  9.5 0.8 %collective-permute-start = (s32[2]{0:T(128)S(1)}, s32[2]{0:T(128)S(1)}, u32[]{:S(2)}, u32[]{:S(2)}) collective-permute-start(s32[2]{0:T(128)S(1)} %get-tuple-element.11), channel_id=1, source_target_pairs={{0,16},{16,32},{32,48},{48,64},{64,80},{80,96},{96,112},{112,0},{1... | collective-permute-start | bytes 32 | tf_op jit(solution)/shard_map/ppermute | solution.py:24
  10.3 2.8 %collective-permute-start.1 = (s32[2]{0:T(128)S(1)}, s32[2]{0:T(128)S(1)}, u32[]{:S(2)}, u32[]{:S(2)}) collective-permute-start(s32[2]{0:T(128)S(1)} %get-tuple-element.12), channel_id=1, source_target_pairs={{0,112},{16,0},{32,16},{48,32},{64,48},{80,64},{96,80},{112,96},{1... | collective-permute-start | bytes 32 | tf_op jit(solution)/shard_map/ppermute | solution.py:24
  13.1 0.1 and_select_fusion.shifts
  13.9 0.5 collective-permute-done
  14.3 0.0 collective-permute-done.1
  14.4 6.5 %all-to-all-done = f32[16,4,16,128]{3,2,1,0:T(8,128)S(1)} async-done(((f32[16,4,16,128]{3,2,1,0:T(8,128)}), f32[16,4,16,128]{3,2,1,0:T(8,128)S(1)}, u32[]{:S(2)}, u32[]{:S(2)}) %all-to-all-start) | async-done | bytes 524320 | tf_op jit(solution)/shard_map/all_to_all | solution.py:409
  20.9 3.0 %collective-permute-start.3 = (f32[16,4,2,128]{3,2,1,0:T(2,128)S(1)}, f32[16,4,2,128]{3,2,1,0:T(2,128)S(1)}, u32[]{:S(2)}, u32[]{:S(2)}) collective-permute-start(f32[16,4,2,128]{3,2,1,0:T(2,128)S(1)} %get-tuple-element.9), channel_id=1, source_target_pairs={{0,112},{16,0},{32,16},{48,32},{64,48},{80,64},{96,80},{112,96},{1... | collective-permute-start | bytes 196616 | tf_op jit(solution)/shard_map/ppermute | solution.py:24
  23.9 0.0 collective-permute-start.2
  23.9 0.1 and_select_fusion.1.shifts
  24.0 3.0 %turn_own.1 = (f32[16,88,128]{2,1,0:T(8,128)}, f32[8,16,128]{2,1,0:T(8,128)S(1)}) custom-call(s32[18]{0:T(128)S(1)} %and_select_fusion.shifts, f32[16,64,128]{2,1,0:T(8,128)S(1)} %bitcast.10), custom_call_target="tpu_custom_call" | custom-call | flops 4000000 | bytes 4000000 | tf_op jit(solution)/shard_map/turn_own/pallas_call | solution.py:425
  27.0 0.0 collective-permute-done.3
  27.0 2.1 %collective-permute-done.2 = f32[16,4,2,128]{3,2,1,0:T(2,128)S(1)} collective-permute-done((f32[16,4,2,128]{3,2,1,0:T(2,128)S(1)}, f32[16,4,2,128]{3,2,1,0:T(2,128)S(1)}, u32[]{:S(2)}, u32[]{:S(2)}) %collective-permute-start.2) | collective-permute-done | bytes 65568 | tf_op jit(solution)/shard_map/ppermute | solution.py:24
  29.1 1.4 %turn_ghost.1 = f32[16,88,128]{2,1,0:T(8,128)} custom-call(s32[20]{0:T(128)S(1)} %and_select_fusion.1.shifts, f32[16,8,128]{2,1,0:T(8,128)S(1)} %bitcast.12, f32[16,8,128]{2,1,0:T(8,128)S(1)} %bitcast.11, f32[8,16,128]{2,1,0:T(8,128)S(1)} %get-tuple-element.7.strips_in, f32[16,88,128]{2,1,0:T(8,128)} %get-tuple-element.8.chunk), custom_call_target="tpu_custom_call", output_to_operand_aliasing={{}: (4, {})} | custom-call | tf_op jit(solution)/shard_map/turn_ghost/pallas_call | solution.py:428
  30.5 5.9 %all-to-all-start.1 = ((f32[16,88,128]{2,1,0:T(8,128)}), f32[16,88,128]{2,1,0:T(8,128)S(1)}, u32[]{:S(2)}, u32[]{:S(2)}) async-start(f32[16,88,128]{2,1,0:T(8,128)} %turn_ghost.1), calls=%async_computation.1 | async-start | bytes 1441792 | tf_op jit(solution)/shard_map/all_to_all | solution.py:435
  36.5 0.0 copy-start
  36.5 0.6 %copy-done = f32[128]{0:T(128)S(1)} copy-done((f32[128]{0:T(128)S(1)}, f32[128]{0:T(128)}, u32[]{:S(2)}) %copy-start) | copy-done | bytes 536
  37.1 0.1 fusion.4
  37.2 0.1 pad_maximum_fusion
  37.3 0.1 dynamic_slice.3.residual
  37.3 13.0 %all-to-all-done.1 = f32[16,88,128]{2,1,0:T(8,128)S(1)} async-done(((f32[16,88,128]{2,1,0:T(8,128)}), f32[16,88,128]{2,1,0:T(8,128)S(1)}, u32[]{:S(2)}, u32[]{:S(2)}) %all-to-all-start.1) | async-done | bytes 720928 | tf_op jit(solution)/shard_map/all_to_all | solution.py:435
  50.3 4.6 %two_sections.1 = f32[64,16,128]{2,1,0:T(8,128)} custom-call(f32[20]{0:T(128)S(1)} %dynamic_slice.3.residual, f32[1408,128]{1,0:T(8,128)S(1)} %bitcast.9), custom_call_target="tpu_custom_call" | custom-call | tf_op jit(solution)/shard_map/two_sections/pallas_call | solution.py:438
  (3 shorter events, 0.1 us)
Async XLA Ops:
  0.0 9.4 %copy-start.1 = (s32[16]{0:T(128)S(1)}, s32[16]{0:T(128)}, u32[]{:S(2)}) copy-start(s32[16]{0:T(128)} %param.6) | copy-start | bytes 196
  0.0 20.8 %all-to-all-start = ((f32[16,4,16,128]{3,2,1,0:T(8,128)}), f32[16,4,16,128]{3,2,1,0:T(8,128)S(1)}, u32[]{:S(2)}, u32[]{:S(2)}) async-start(f32[16,4,16,128]{3,2,1,0:T(8,128)} %bitcast.13), calls=%async_computation | async-start | bytes 1048576 | tf_op jit(solution)/shard_map/all_to_all | solution.py:409
  9.5 4.8 %collective-permute-start = (s32[2]{0:T(128)S(1)}, s32[2]{0:T(128)S(1)}, u32[]{:S(2)}, u32[]{:S(2)}) collective-permute-start(s32[2]{0:T(128)S(1)} %get-tuple-element.11), channel_id=1, source_target_pairs={{0,16},{16,32},{32,48},{48,64},{64,80},{80,96},{96,112},{112,0},{1... | collective-permute-start | bytes 32 | tf_op jit(solution)/shard_map/ppermute | solution.py:24
  10.3 4.1 %collective-permute-start.1 = (s32[2]{0:T(128)S(1)}, s32[2]{0:T(128)S(1)}, u32[]{:S(2)}, u32[]{:S(2)}) collective-permute-start(s32[2]{0:T(128)S(1)} %get-tuple-element.12), channel_id=1, source_target_pairs={{0,112},{16,0},{32,16},{48,32},{64,48},{80,64},{96,80},{112,96},{1... | collective-permute-start | bytes 32 | tf_op jit(solution)/shard_map/ppermute | solution.py:24
  20.9 6.1 %collective-permute-start.3 = (f32[16,4,2,128]{3,2,1,0:T(2,128)S(1)}, f32[16,4,2,128]{3,2,1,0:T(2,128)S(1)}, u32[]{:S(2)}, u32[]{:S(2)}) collective-permute-start(f32[16,4,2,128]{3,2,1,0:T(2,128)S(1)} %get-tuple-element.9), channel_id=1, source_target_pairs={{0,112},{16,0},{32,16},{48,32},{64,48},{80,64},{96,80},{112,96},{1... | collective-permute-start | bytes 196616 | tf_op jit(solution)/shard_map/ppermute | solution.py:24
  23.9 5.2 %collective-permute-start.2 = (f32[16,4,2,128]{3,2,1,0:T(2,128)S(1)}, f32[16,4,2,128]{3,2,1,0:T(2,128)S(1)}, u32[]{:S(2)}, u32[]{:S(2)}) collective-permute-start(f32[16,4,2,128]{3,2,1,0:T(2,128)S(1)} %get-tuple-element.10), channel_id=1, source_target_pairs={{0,16},{16,32},{32,48},{48,64},{64,80},{80,96},{96,112},{112,0},{1... | collective-permute-start | bytes 196616 | tf_op jit(solution)/shard_map/ppermute | solution.py:24
  30.5 19.7 %all-to-all-start.1 = ((f32[16,88,128]{2,1,0:T(8,128)}), f32[16,88,128]{2,1,0:T(8,128)S(1)}, u32[]{:S(2)}, u32[]{:S(2)}) async-start(f32[16,88,128]{2,1,0:T(8,128)} %turn_ghost.1), calls=%async_computation.1 | async-start | bytes 1441792 | tf_op jit(solution)/shard_map/all_to_all | solution.py:435
  36.5 0.7 %copy-start = (f32[128]{0:T(128)S(1)}, f32[128]{0:T(128)}, u32[]{:S(2)}) copy-start(f32[128]{0:T(128)} %param.5) | copy-start | bytes 1540

commit v3 on v2

--- a/solution.py
+++ b/solution.py
@@ -67,7 +67,7 @@
             wide_row = row + DEPTH
             for plane in range(planes):
                 line = plane * rows + row
-                window, rim, part = turned_line(flat, line, own, groups, shifts[wide_row], lane)
+                window, rim, part = turned_line(flat, line, own, groups, shifts[row], lane)
                 target[pl.ds(line, groups, stride=own), :] = window
                 strips[wide_row % 2][plane] = placed_strip(
                     rim, part, wide_row // 2, lane, strips[wide_row % 2][plane]
@@ -103,7 +103,8 @@
     ghost = DEPTH * planes
     zone = 3 * ghost
 
-    def kernel(shifts, low, high, strips_in, chunk, out, lines, windows, sems):
+    def kernel(shift_tiles, low, high, strips_in, chunk, out, lines, windows, sems):
+        amounts = [jnp.max(shift_tiles[entry]) for entry in range(2 * DEPTH)]
         lay_twice(low, lines, 0, ghost, groups)
         lay_twice(high, lines, ghost, ghost, groups)
         flat = lines.reshape((2 * groups + 1) * 2 * ghost, LANES)
@@ -127,7 +128,7 @@
                 for plane in range(planes):
                     line = side * ghost + plane * DEPTH + row
                     window, rim, part = turned_line(
-                        flat, line, 2 * ghost, groups, shifts[wide_row], lane
+                        flat, line, 2 * ghost, groups, amounts[side * DEPTH + row], lane
                     )
                     place = side * groups * ghost + plane * DEPTH + row
                     target[pl.ds(place, groups, stride=ghost), :] = window
@@ -145,8 +146,7 @@
 
     return pl.pallas_call(
         kernel,
-        in_specs=[pl.BlockSpec(memory_space=pltpu.SMEM)]
-        + [pl.BlockSpec(memory_space=pltpu.VMEM)] * 3
+        in_specs=[pl.BlockSpec(memory_space=pltpu.VMEM)] * 4
         + [pl.BlockSpec(memory_space=pl.ANY)],
         out_shape=jax.ShapeDtypeStruct((groups, own + zone, LANES), jnp.float32),
         out_specs=pl.BlockSpec(memory_space=pl.ANY),
@@ -177,98 +177,116 @@
     return pltpu.roll(tile, 1, 0)
 
 
-def radial_edges(prev, here, drift_prev, drift):
+def low_side(here, residual):
+    vel_y = y_dn(here[2])
+    return y_dn(here[1]), vel_y + residual, y_dn(here[5]), vel_y
+
+
+def radial_edges(prev, here, drift_prev, drift, low_prev, low):
     _, vel_x, _, vel_z, _, mag_x, mag_y, mag_z = here
     two_x = vel_x + prev[1]
     two_z = vel_z + prev[3]
     two_w = drift + drift_prev
-    mag_x_y = y_dn(mag_x)
+    four_x = two_x + (low[0] + low_prev[0])
+    four_w = two_w + (low[1] + low_prev[1])
     mag_x_z = z_dn(mag_x)
-    emf_z = 0.125 * (
-        (two_w + y_dn(two_w)) * (mag_x + mag_x_y) - (two_x + y_dn(two_x)) * (mag_y + prev[6])
-    ) + resist * ((mag_y - prev[6]) - (mag_x - mag_x_y))
-    emf_y = 0.125 * (
+    emf_z = (0.125 * time_step) * (four_w * (mag_x + low[2]) - four_x * (mag_y + prev[6])) + (time_step * resist) * (
+        (mag_y - prev[6]) - (mag_x - low[2])
+    )
+    emf_y = (0.125 * time_step) * (
         (two_x + z_dn(two_x)) * (mag_z + prev[7]) - (two_z + z_dn(two_z)) * (mag_x + mag_x_z)
-    ) + resist * ((mag_x - mag_x_z) - (mag_z - prev[7]))
+    ) + (time_step * resist) * ((mag_x - mag_x_z) - (mag_z - prev[7]))
     return emf_z, emf_y
 
 
-def row_rates(prev, here, after, residual, edges, edges_after):
+def row_step(prev, here, after, residual, low, low_after, edges, edges_after):
     log_rho, vel_x, vel_y, vel_z, entropy, mag_x, mag_y, mag_z = here
     drift = vel_y + residual
-    half_x = 0.5 * vel_x
-    half_w = 0.5 * drift
-    half_z = 0.5 * vel_z
-
-    def moved_by(index):
+    half_x = (0.5 * time_step) * vel_x
+    half_w = (0.5 * time_step) * drift
+    half_z = (0.5 * time_step) * vel_z
+
+    def moved_by(index, left=None):
         center = here[index]
         fore, back = after[index], prev[index]
-        left, right = y_dn(center), y_up(center)
+        left = y_dn(center) if left is None else left
+        right = y_up(center)
         under, over = z_dn(center), z_up(center)
         d_x, d_y, d_z = fore - back, right - left, over - under
         total = ((fore + back) + (left + right)) + (under + over)
-        rate = viscous * total - (6.0 * viscous) * center
-        rate = rate - (half_x * d_x + half_w * d_y + half_z * d_z)
-        return rate, d_x, d_y, d_z, left
-
-    rate_l, l_x, l_y, l_z, _ = moved_by(0)
-    rate_vx, vx_x, _, _, _ = moved_by(1)
-    rate_vy, _, vy_y, _, vy_left = moved_by(2)
-    rate_vz, _, _, vz_z, vz_left = moved_by(3)
-    rate_s, s_x, s_y, s_z, _ = moved_by(4)
+        result = (time_step * viscous) * total + (1.0 - 6.0 * time_step * viscous) * center
+        result = result - (half_x * d_x + half_w * d_y + half_z * d_z)
+        return result, d_x, d_y, d_z, left
+
+    next_l, l_x, l_y, l_z, _ = moved_by(0)
+    next_vx, vx_x, _, _, _ = moved_by(1, low[0])
+    next_vy, _, vy_y, _, _ = moved_by(2, low[3])
+    next_vz, _, _, vz_z, vz_left = moved_by(3)
+    next_s, s_x, s_y, s_z, _ = moved_by(4)
 
     two_bx = mag_x + after[5]
     two_by = mag_y + y_up(mag_y)
     two_bz = mag_z + z_up(mag_z)
-    two_bx_left = y_dn(two_bx)
+    two_bx_left = low[2] + low_after[2]
+    mag_z_y = y_dn(mag_z)
     diff_y = after[6] - prev[6]
     diff_z = after[7] - prev[7]
-    cur_x = (y_up(two_bz) - y_dn(two_bz)) - (z_up(two_by) - z_dn(two_by))
+    cur_x = (y_up(two_bz) - (mag_z_y + z_up(mag_z_y))) - (z_up(two_by) - z_dn(two_by))
     cur_y = (z_up(two_bx) - z_dn(two_bx)) - (diff_z + z_up(diff_z))
-    cur_z = (diff_y + y_up(diff_y)) - (y_up(two_bx) - two_bx_left)
+    cur_z = (diff_y + two_bx_left) + y_up(diff_y - two_bx)
     inverse = jnp.exp(-log_rho)
-    eighth = 0.125 * inverse
-    rate_l = rate_l - 0.5 * (vx_x + vy_y + vz_z)
-    rate_vx = (
-        rate_vx
-        - (0.5 * sound_sq) * (l_x + s_x)
+    eighth = (0.125 * time_step) * inverse
+    next_l = next_l - (0.5 * time_step) * (vx_x + vy_y + vz_z)
+    next_vx = (
+        next_vx
+        - (0.5 * time_step * sound_sq) * (l_x + s_x)
         + eighth * (cur_y * two_bz - cur_z * two_by)
-        + (2.0 * rotation) * vel_y
-    )
-    rate_vy = (
-        rate_vy
-        - (0.5 * sound_sq) * (l_y + s_y)
+        + (2.0 * time_step * rotation) * vel_y
+    )
+    next_vy = (
+        next_vy
+        - (0.5 * time_step * sound_sq) * (l_y + s_y)
         + eighth * (cur_z * two_bx - cur_x * two_bz)
-        - ((2.0 - shear_rate) * rotation) * vel_x
-    )
-    rate_vz = (
-        rate_vz
-        - (0.5 * sound_sq) * (l_z + s_z)
+        - (time_step * (2.0 - shear_rate) * rotation) * vel_x
+    )
+    next_vz = (
+        next_vz
+        - (0.5 * time_step * sound_sq) * (l_z + s_z)
         + eighth * (cur_x * two_by - cur_y * two_bx)
     )
-    rate_s = rate_s + (resist * 0.0625) * inverse * (cur_x * cur_x + cur_y * cur_y + cur_z * cur_z)
+    next_s = next_s + (0.0625 * time_step * resist) * inverse * (cur_x * cur_x + cur_y * cur_y + cur_z * cur_z)
 
     emf_z, emf_y = edges
     emf_z_after, emf_y_after = edges_after
-    pair_w = drift + (vy_left + residual_left(residual))
+    pair_w = drift + low[1]
     pair_z = vel_z + vz_left
-    mag_z_y = y_dn(mag_z)
     mag_y_z = z_dn(mag_y)
-    emf_x = 0.125 * (
+    emf_x = (0.125 * time_step) * (
         (pair_z + z_dn(pair_z)) * (mag_y + mag_y_z) - (pair_w + z_dn(pair_w)) * (mag_z + mag_z_y)
-    ) + resist * ((mag_z - mag_z_y) - (mag_y - mag_y_z))
-    rate_bx = (emf_z - y_up(emf_z)) + (z_up(emf_y) - emf_y)
-    rate_by = (
-        (emf_x - z_up(emf_x))
+    ) + (time_step * resist) * ((mag_z - mag_z_y) - (mag_y - mag_y_z))
+    next_bx = mag_x + (emf_z - y_up(emf_z)) + (z_up(emf_y) - emf_y)
+    next_by = (
+        mag_y
+        + (emf_x - z_up(emf_x))
         + (emf_z_after - emf_z)
-        - (0.25 * shear_rate * rotation) * (two_bx + two_bx_left)
-    )
-    rate_bz = (emf_y - emf_y_after) + (y_up(emf_x) - emf_x)
-    return [rate_l, rate_vx, rate_vy, rate_vz, rate_s, rate_bx, rate_by, rate_bz]
-
-
-def residual_left(residual):
-    return residual
+        - (0.25 * time_step * shear_rate * rotation) * (two_bx + two_bx_left)
+    )
+    next_bz = mag_z + (emf_y - emf_y_after) + (y_up(emf_x) - emf_x)
+    return [next_l, next_vx, next_vy, next_vz, next_s, next_bx, next_by, next_bz]
+
+
+def drift_tiles(drift, depth):
+    wide = drift.shape[0]
+    pairs = jnp.broadcast_to(drift.reshape(wide // 2, 2, 1), (wide // 2, 2, STRIP))
+    strips = jnp.pad(
+        jnp.swapaxes(pairs, 0, 1).reshape(2, wide // 2 * STRIP),
+        ((0, 0), (0, LANES - wide // 2 * STRIP)),
+    )
+    strips = jnp.stack(
+        [jnp.roll(strips[1], STRIP), strips[0], strips[1], jnp.roll(strips[0], -STRIP)]
+    )
+    tiles = jnp.concatenate([jnp.broadcast_to(drift[:, None], (wide, LANES)), strips])
+    return jnp.broadcast_to(tiles[:, None], (wide + 4, depth, LANES))
 
 
 def two_sections(fields, depth, rows):
@@ -279,7 +297,7 @@
     chunk = own + 3 * ghost
     strip_at = wide
 
-    def kernel(residual, source, out, moved, first, drift_rows, ends, evolved, sems):
+    def kernel(drift_rows, source, out, moved, first, ends, evolved, sems):
         flat_out = evolved.reshape(fields * depth * rows, LANES)
         lane = lax.broadcasted_iota(jnp.int32, (depth, LANES), 1)
 
@@ -290,15 +308,6 @@
                 ref[field, strip_at] = pltpu.roll(odd, STRIP, 1)
                 ref[field, strip_at + 3] = pltpu.roll(even, LANES - STRIP, 1)
 
-        strip_drift = [jnp.zeros((depth, LANES), jnp.float32) for _ in range(2)]
-        for row in range(wide):
-            value = jnp.full((depth, LANES), residual[row], jnp.float32)
-            drift_rows[row] = value
-            strip_drift[row % 2] = jnp.where(lane // STRIP == row // 2, value, strip_drift[row % 2])
-        drift_rows[strip_at] = pltpu.roll(strip_drift[1], STRIP, 1)
-        drift_rows[strip_at + 1] = strip_drift[0]
-        drift_rows[strip_at + 2] = strip_drift[1]
-        drift_rows[strip_at + 3] = pltpu.roll(strip_drift[0], LANES - STRIP, 1)
         under = lax.broadcasted_iota(jnp.int32, (depth, LANES), 0) < half
 
         def column(first, stride):
@@ -324,17 +333,21 @@
 
         def edges_of(ref, row):
             prev, here = row_of(ref, row - 1), row_of(ref, row)
-            return radial_edges(
-                prev, here, prev[2] + drift_rows[row - 1], here[2] + drift_rows[row]
+            drift_prev, drift = prev[2] + drift_rows[row - 1], here[2] + drift_rows[row]
+            low = low_side(here, drift_rows[row])
+            low_prev = low_side(prev, drift_rows[row - 1])
+            return low, radial_edges(prev, here, drift_prev, drift, low_prev, low)
+
+        def step(ref, row, carried):
+            low, edges = carried
+            prev, here, after = row_of(ref, row - 1), row_of(ref, row), row_of(ref, row + 1)
+            drift, drift_after = here[2] + drift_rows[row], after[2] + drift_rows[row + 1]
+            low_after = low_side(after, drift_rows[row + 1])
+            edges_after = radial_edges(here, after, drift, drift_after, low, low_after)
+            result = row_step(
+                prev, here, after, drift_rows[row], low, low_after, edges, edges_after
             )
-
-        def step(ref, row, edges):
-            prev, here, after = row_of(ref, row - 1), row_of(ref, row), row_of(ref, row + 1)
-            edges_after = radial_edges(
-                here, after, here[2] + drift_rows[row], after[2] + drift_rows[row + 1]
-            )
-            rate = row_rates(prev, here, after, drift_rows[row], edges, edges_after)
-            return [a + time_step * b for a, b in zip(here, rate)], edges_after
+            return result, (low_after, edges_after)
 
         def first_row(row, edges):
             result, edges = step(moved, row, edges)
@@ -346,7 +359,7 @@
         for row in (strip_at + 1, strip_at + 2):
             edges = first_row(row, edges)
         widen_strips(first)
-        lax.fori_loop(1, wide - 1, first_row, edges_of(moved, 1), unroll=3)
+        lax.fori_loop(1, wide - 1, first_row, edges_of(moved, 1), unroll=6)
 
         edges = edges_of(first, strip_at + 1)
         for parity in range(2):
@@ -381,13 +394,12 @@
 
     return pl.pallas_call(
         kernel,
-        in_specs=[pl.BlockSpec(memory_space=pltpu.SMEM), pl.BlockSpec(memory_space=pltpu.VMEM)],
+        in_specs=[pl.BlockSpec(memory_space=pltpu.VMEM), pl.BlockSpec(memory_space=pltpu.VMEM)],
         out_shape=jax.ShapeDtypeStruct((fields * depth, rows, LANES), jnp.float32),
         out_specs=pl.BlockSpec(memory_space=pl.ANY),
         scratch_shapes=[
             pltpu.VMEM((fields, wide + 4, depth, LANES), jnp.float32),
             pltpu.VMEM((fields, wide + 4, depth, LANES), jnp.float32),
-            pltpu.VMEM((wide + 4, depth, LANES), jnp.float32),
             pltpu.VMEM((fields, 2, depth, LANES), jnp.float32),
             pltpu.VMEM((fields * depth, rows, LANES), jnp.float32),
             pltpu.SemaphoreType.DMA((rows // TILE_ROWS, fields)),
@@ -413,20 +425,20 @@
     high = passed_along(lines[:, :, :DEPTH], "gx", -1)
     low_shift = passed_along(shift_rows[rows - DEPTH :], "gx", 1)
     high_shift = passed_along(shift_rows[:DEPTH], "gx", -1)
-    shifts = jnp.concatenate(
+    ghost_shifts = jnp.concatenate(
         [
             low_shift - jnp.where(row_dev == 0, offset, 0),
-            shift_rows,
             high_shift + jnp.where(row_dev == radial_count - 1, offset, 0),
         ]
     )
-    shifts = (shifts + DEPTH) % cells_y
-    own_shifts = jnp.concatenate([shift_rows[:DEPTH], shift_rows]) + DEPTH
+    ghost_shifts = (ghost_shifts + DEPTH) % cells_y
+    ghost_shifts = jnp.broadcast_to(ghost_shifts[:, None, None], (2 * DEPTH, TILE_ROWS, LANES))
+    own_shifts = shift_rows + DEPTH
     chunk, strips = turn_own(groups, rows, planes)(
         own_shifts % cells_y, lines.reshape(groups, planes * rows, cols)
     )
     chunk = turn_ghost(groups, rows, planes)(
-        shifts,
+        ghost_shifts,
         low.reshape(groups, planes * DEPTH, cols),
         high.reshape(groups, planes * DEPTH, cols),
         strips,
@@ -435,7 +447,9 @@
     wide = lax.all_to_all(chunk, "gy", split_axis=0, concat_axis=0, tiled=True)
     padded = jnp.concatenate([residual[-DEPTH:], residual, residual[:DEPTH]])
     drift = lax.dynamic_slice_in_dim(padded, row_dev * rows, rows + 2 * DEPTH)
-    evolved = two_sections(fields, depth, rows)(drift, wide.reshape(-1, cols))
+    evolved = two_sections(fields, depth, rows)(
+        drift_tiles(drift, depth), wide.reshape(-1, cols)
+    )
     return evolved.reshape(state.shape)
 
 

time: 55.2 us -> 53.7 us (0.973)
  Pallas kernels: 8.98 us -> 7.51 us
    pallas_call x1, Pallas kernels: 4.55 us -> 3.4 us  [local(): two_sections(fields, depth, rows)]
    unnamed x4, local copies, waits for them, and re-layouts: 0.65 us -> 0.01 us
  transfers between devices with their start and end apart: 6 -> 6, of which waited for: 4 -> 4; matrix products, arithmetic and copies ran while one was open for 1% -> 2% of each run, Pallas kernels for 5% -> 6%
where the time goes in v3:
time: 53.7 us; the launch traced here: 53.4 us
  waiting for transfers between devices  22.2 us (41%)
  starting transfers between devices  22 us (41%)
  Pallas kernels  7.51 us (14%)
  local copies, waits for them, and re-layouts  0.76 us (1%)
  between operations  0.71 us (1%)
    all_to_all x1, waiting for transfers between devices, local(): wide = lax.all_to_all(chunk, 'gy', split_axis=0, concat_axis=0, tiled=True)  13.4 us
    all_to_all x1, starting transfers between devices, local(): lax.all_to_all(state.reshape(groups, planes, rows, cols), 'gy', split_axi...  9.43 us
    ppermute x4, starting transfers between devices, passed_along(): return lax.ppermute(value, axis, pairs)  6.61 us
    all_to_all x1, waiting for transfers between devices, local(): lax.all_to_all(state.reshape(groups, planes, rows, cols), 'gy', split_axi...  6.47 us
    all_to_all x1, starting transfers between devices, local(): wide = lax.all_to_all(chunk, 'gy', split_axis=0, concat_axis=0, tiled=True)  5.91 us
    pallas_call x1, Pallas kernels, local(): two_sections(fields, depth, rows)  3.4 us
    pallas_call x1, Pallas kernels, local(): turn_own(groups, rows, planes)  3.03 us
    ppermute x4, waiting for transfers between devices, passed_along(): return lax.ppermute(value, axis, pairs)  2.24 us
  transfers between devices with their start and end apart: 6, of which 4 were waited for; matrix products, arithmetic and copies ran while one was open for 2% of the time, Pallas kernels for 6%

profile of v3, /device:TPU:1, one launch (start us, length us, event | category | flops | bytes accessed | tf_op | source)
XLA Modules:
  0.0 53.4 jit_solution(17807992207601307920)
XLA Ops:
  0.0 0.0 copy-start.1
  0.0 9.4 %all-to-all-start = ((f32[16,4,16,128]{3,2,1,0:T(8,128)}), f32[16,4,16,128]{3,2,1,0:T(8,128)S(1)}, u32[]{:S(2)}, u32[]{:S(2)}) async-start(f32[16,4,16,128]{3,2,1,0:T(8,128)} %bitcast.25), calls=%async_computation | async-start | bytes 1048576 | tf_op jit(solution)/shard_map/all_to_all | solution.py:421
  9.4 0.0 copy-done.1
  9.4 0.1 fusion.3
  9.5 0.8 %collective-permute-start = (s32[2]{0:T(128)S(1)}, s32[2]{0:T(128)S(1)}, u32[]{:S(2)}, u32[]{:S(2)}) collective-permute-start(s32[2]{0:T(128)S(1)} %get-tuple-element.13), channel_id=1, source_target_pairs={{0,16},{16,32},{32,48},{48,64},{64,80},{80,96},{96,112},{112,0},{1... | collective-permute-start | bytes 32 | tf_op jit(solution)/shard_map/ppermute | solution.py:24
  10.3 0.0 copy-start
  10.3 2.8 %collective-permute-start.1 = (s32[2]{0:T(128)S(1)}, s32[2]{0:T(128)S(1)}, u32[]{:S(2)}, u32[]{:S(2)}) collective-permute-start(s32[2]{0:T(128)S(1)} %get-tuple-element.14), channel_id=1, source_target_pairs={{0,112},{16,0},{32,16},{48,32},{64,48},{80,64},{96,80},{112,96},{1... | collective-permute-start | bytes 32 | tf_op jit(solution)/shard_map/ppermute | solution.py:24
  13.1 0.0 copy-done
  13.1 0.1 fusion.4
  13.2 0.1 pad_maximum_fusion.1
  13.9 0.1 dynamic_slice.3
  14.0 0.1 broadcast_in_dim.11
  14.1 0.1 copy.7
  14.2 0.1 collective-permute-done
  14.3 0.0 collective-permute-done.1
  14.4 6.5 %all-to-all-done = f32[16,4,16,128]{3,2,1,0:T(8,128)S(1)} async-done(((f32[16,4,16,128]{3,2,1,0:T(8,128)}), f32[16,4,16,128]{3,2,1,0:T(8,128)S(1)}, u32[]{:S(2)}, u32[]{:S(2)}) %all-to-all-start) | async-done | bytes 524320 | tf_op jit(solution)/shard_map/all_to_all | solution.py:421
  20.9 3.0 %collective-permute-start.3 = (f32[16,4,2,128]{3,2,1,0:T(2,128)S(1)}, f32[16,4,2,128]{3,2,1,0:T(2,128)S(1)}, u32[]{:S(2)}, u32[]{:S(2)}) collective-permute-start(f32[16,4,2,128]{3,2,1,0:T(2,128)S(1)} %get-tuple-element.9), channel_id=1, source_target_pairs={{0,112},{16,0},{32,16},{48,32},{64,48},{80,64},{96,80},{112,96},{1... | collective-permute-start | bytes 196616 | tf_op jit(solution)/shard_map/ppermute | solution.py:24
  23.9 0.0 collective-permute-start.2
  23.9 0.1 and_select_fusion.1
  24.0 3.0 %turn_own.1 = (f32[16,88,128]{2,1,0:T(8,128)}, f32[8,16,128]{2,1,0:T(8,128)S(1)}) custom-call(s32[16]{0:T(128)S(1)} %and_select_fusion.shifts, f32[16,64,128]{2,1,0:T(8,128)S(1)} %bitcast.22), custom_call_target="tpu_custom_call" | custom-call | flops 4000000 | bytes 4000000 | tf_op jit(solution)/shard_map/turn_own/pallas_call | solution.py:437
  27.0 0.0 collective-permute-done.3
  27.0 2.1 %collective-permute-done.2 = f32[16,4,2,128]{3,2,1,0:T(2,128)S(1)} collective-permute-done((f32[16,4,2,128]{3,2,1,0:T(2,128)S(1)}, f32[16,4,2,128]{3,2,1,0:T(2,128)S(1)}, u32[]{:S(2)}, u32[]{:S(2)}) %collective-permute-start.2) | collective-permute-done | bytes 65568 | tf_op jit(solution)/shard_map/ppermute | solution.py:24
  29.1 0.1 broadcast_in_dim.14.shift_tiles
  29.2 1.1 %turn_ghost.1 = f32[16,88,128]{2,1,0:T(8,128)} custom-call(s32[4,8,128]{2,1,0:T(8,128)S(1)} %broadcast_in_dim.14.shift_tiles, f32[16,8,128]{2,1,0:T(8,128)S(1)} %bitcast.24, f32[16,8,128]{2,1,0:T(8,128)S(1)} %bitcast.23, f32[8,16,128]{2,1,0:T(8,128)S(1)} %get-tuple-element.7.strips_in, ...), custom_call_target="tpu_custom_call", output_to_operand_aliasing={{}: (4, {})} | custom-call | tf_op jit(solution)/shard_map/turn_ghost/pallas_call | solution.py:440
  30.3 5.9 %all-to-all-start.1 = ((f32[16,88,128]{2,1,0:T(8,128)}), f32[16,88,128]{2,1,0:T(8,128)S(1)}, u32[]{:S(2)}, u32[]{:S(2)}) async-start(f32[16,88,128]{2,1,0:T(8,128)} %turn_ghost.1), calls=%async_computation.1 | async-start | bytes 1441792 | tf_op jit(solution)/shard_map/all_to_all | solution.py:447
  36.2 0.1 broadcast_bitcast_fusion
  36.2 0.1 reshape.55
  36.3 0.1 slice_bitcast_fusion.2
  36.4 0.1 maximum_bitcast_fusion
  36.5 0.1 pad_maximum_fusion
  36.6 13.4 %all-to-all-done.1 = f32[16,88,128]{2,1,0:T(8,128)S(1)} async-done(((f32[16,88,128]{2,1,0:T(8,128)}), f32[16,88,128]{2,1,0:T(8,128)S(1)}, u32[]{:S(2)}, u32[]{:S(2)}) %all-to-all-start.1) | async-done | bytes 720928 | tf_op jit(solution)/shard_map/all_to_all | solution.py:447
  50.0 3.4 %two_sections.1 = f32[64,16,128]{2,1,0:T(8,128)} custom-call(f32[24,8,128]{2,1,0:T(8,128)S(1)} %broadcast_in_dim.13.drift_rows, f32[1408,128]{1,0:T(8,128)S(1)} %bitcast.21), custom_call_target="tpu_custom_call" | custom-call | tf_op jit(solution)/shard_map/two_sections/pallas_call | solution.py:450
  (8 shorter events, 0.1 us)
Async XLA Ops:
  0.0 9.4 %copy-start.1 = (s32[16]{0:T(128)S(1)}, s32[16]{0:T(128)}, u32[]{:S(2)}) copy-start(s32[16]{0:T(128)} %param.6) | copy-start | bytes 196
  0.0 20.8 %all-to-all-start = ((f32[16,4,16,128]{3,2,1,0:T(8,128)}), f32[16,4,16,128]{3,2,1,0:T(8,128)S(1)}, u32[]{:S(2)}, u32[]{:S(2)}) async-start(f32[16,4,16,128]{3,2,1,0:T(8,128)} %bitcast.25), calls=%async_computation | async-start | bytes 1048576 | tf_op jit(solution)/shard_map/all_to_all | solution.py:421
  9.5 4.8 %collective-permute-start = (s32[2]{0:T(128)S(1)}, s32[2]{0:T(128)S(1)}, u32[]{:S(2)}, u32[]{:S(2)}) collective-permute-start(s32[2]{0:T(128)S(1)} %get-tuple-element.13), channel_id=1, source_target_pairs={{0,16},{16,32},{32,48},{48,64},{64,80},{80,96},{96,112},{112,0},{1... | collective-permute-start | bytes 32 | tf_op jit(solution)/shard_map/ppermute | solution.py:24
  10.3 2.9 %copy-start = (f32[128]{0:T(128)S(1)}, f32[128]{0:T(128)}, u32[]{:S(2)}) copy-start(f32[128]{0:T(128)} %param.5) | copy-start | bytes 1540
  10.3 4.1 %collective-permute-start.1 = (s32[2]{0:T(128)S(1)}, s32[2]{0:T(128)S(1)}, u32[]{:S(2)}, u32[]{:S(2)}) collective-permute-start(s32[2]{0:T(128)S(1)} %get-tuple-element.14), channel_id=1, source_target_pairs={{0,112},{16,0},{32,16},{48,32},{64,48},{80,64},{96,80},{112,96},{1... | collective-permute-start | bytes 32 | tf_op jit(solution)/shard_map/ppermute | solution.py:24
  20.9 6.1 %collective-permute-start.3 = (f32[16,4,2,128]{3,2,1,0:T(2,128)S(1)}, f32[16,4,2,128]{3,2,1,0:T(2,128)S(1)}, u32[]{:S(2)}, u32[]{:S(2)}) collective-permute-start(f32[16,4,2,128]{3,2,1,0:T(2,128)S(1)} %get-tuple-element.9), channel_id=1, source_target_pairs={{0,112},{16,0},{32,16},{48,32},{64,48},{80,64},{96,80},{112,96},{1... | collective-permute-start | bytes 196616 | tf_op jit(solution)/shard_map/ppermute | solution.py:24
  23.9 5.2 %collective-permute-start.2 = (f32[16,4,2,128]{3,2,1,0:T(2,128)S(1)}, f32[16,4,2,128]{3,2,1,0:T(2,128)S(1)}, u32[]{:S(2)}, u32[]{:S(2)}) collective-permute-start(f32[16,4,2,128]{3,2,1,0:T(2,128)S(1)} %get-tuple-element.10), channel_id=1, source_target_pairs={{0,16},{16,32},{32,48},{48,64},{64,80},{80,96},{96,112},{112,0},{1... | collective-permute-start | bytes 196616 | tf_op jit(solution)/shard_map/ppermute | solution.py:24
  30.3 19.7 %all-to-all-start.1 = ((f32[16,88,128]{2,1,0:T(8,128)}), f32[16,88,128]{2,1,0:T(8,128)S(1)}, u32[]{:S(2)}, u32[]{:S(2)}) async-start(f32[16,88,128]{2,1,0:T(8,128)} %turn_ghost.1), calls=%async_computation.1 | async-start | bytes 1441792 | tf_op jit(solution)/shard_map/all_to_all | solution.py:447

commit v4 on v3

--- a/solution.py
+++ b/solution.py
@@ -104,7 +104,8 @@
     zone = 3 * ghost
 
     def kernel(shift_tiles, low, high, strips_in, chunk, out, lines, windows, sems):
-        amounts = [jnp.max(shift_tiles[entry]) for entry in range(2 * DEPTH)]
+        shift_rows = shift_tiles[...]
+        amounts = [shift_rows[entry, 0] for entry in range(2 * DEPTH)]
         lay_twice(low, lines, 0, ghost, groups)
         lay_twice(high, lines, ghost, ghost, groups)
         flat = lines.reshape((2 * groups + 1) * 2 * ghost, LANES)
@@ -425,14 +426,14 @@
     high = passed_along(lines[:, :, :DEPTH], "gx", -1)
     low_shift = passed_along(shift_rows[rows - DEPTH :], "gx", 1)
     high_shift = passed_along(shift_rows[:DEPTH], "gx", -1)
+    across = jnp.ones((1, cols), jnp.int32)
     ghost_shifts = jnp.concatenate(
         [
-            low_shift - jnp.where(row_dev == 0, offset, 0),
-            high_shift + jnp.where(row_dev == radial_count - 1, offset, 0),
+            (low_shift - jnp.where(row_dev == 0, offset, 0))[:, None] * across,
+            (high_shift + jnp.where(row_dev == radial_count - 1, offset, 0))[:, None] * across,
         ]
     )
     ghost_shifts = (ghost_shifts + DEPTH) % cells_y
-    ghost_shifts = jnp.broadcast_to(ghost_shifts[:, None, None], (2 * DEPTH, TILE_ROWS, LANES))
     own_shifts = shift_rows + DEPTH
     chunk, strips = turn_own(groups, rows, planes)(
         own_shifts % cells_y, lines.reshape(groups, planes * rows, cols)

time: 53.7 us -> 53.5 us (level)
  no operation moved by 1% of the time
where the time goes in v4:
time: 53.5 us; the launch traced here: 53.2 us
  waiting for transfers between devices  22.1 us (41%)
  starting transfers between devices  22 us (41%)
  Pallas kernels  7.35 us (14%)
  between operations  0.73 us (1%)
  local copies, waits for them, and re-layouts  0.69 us (1%)
    all_to_all x1, waiting for transfers between devices, local(): wide = lax.all_to_all(chunk, 'gy', split_axis=0, concat_axis=0, tiled=True)  13.4 us
    all_to_all x1, starting transfers between devices, local(): lax.all_to_all(state.reshape(groups, planes, rows, cols), 'gy', split_axi...  9.43 us
    ppermute x4, starting transfers between devices, passed_along(): return lax.ppermute(value, axis, pairs)  6.61 us
    all_to_all x1, waiting for transfers between devices, local(): lax.all_to_all(state.reshape(groups, planes, rows, cols), 'gy', split_axi...  6.39 us
    all_to_all x1, starting transfers between devices, local(): wide = lax.all_to_all(chunk, 'gy', split_axis=0, concat_axis=0, tiled=True)  5.91 us
    pallas_call x1, Pallas kernels, local(): two_sections(fields, depth, rows)  3.4 us
    pallas_call x1, Pallas kernels, local(): turn_own(groups, rows, planes)  3.03 us
    ppermute x4, waiting for transfers between devices, passed_along(): return lax.ppermute(value, axis, pairs)  2.23 us
  transfers between devices with their start and end apart: 6, of which 4 were waited for; matrix products, arithmetic and copies ran while one was open for 2% of the time, Pallas kernels for 6%

profile of v4, /device:TPU:1, one launch (start us, length us, event | category | flops | bytes accessed | tf_op | source)
XLA Modules:
  0.0 53.2 jit_solution(2215716703957161096)
XLA Ops:
  0.0 0.0 copy-start.1
  0.0 9.4 %all-to-all-start = ((f32[16,4,16,128]{3,2,1,0:T(8,128)}), f32[16,4,16,128]{3,2,1,0:T(8,128)S(1)}, u32[]{:S(2)}, u32[]{:S(2)}) async-start(f32[16,4,16,128]{3,2,1,0:T(8,128)} %bitcast.25), calls=%async_computation | async-start | bytes 1048576 | tf_op jit(solution)/shard_map/all_to_all | solution.py:422
  9.4 0.0 copy-done.1
  9.4 0.1 fusion.5
  9.5 0.8 %collective-permute-start = (s32[2]{0:T(128)S(1)}, s32[2]{0:T(128)S(1)}, u32[]{:S(2)}, u32[]{:S(2)}) collective-permute-start(s32[2]{0:T(128)S(1)} %get-tuple-element.15), channel_id=1, source_target_pairs={{0,16},{16,32},{32,48},{48,64},{64,80},{80,96},{96,112},{112,0},{1... | collective-permute-start | bytes 32 | tf_op jit(solution)/shard_map/ppermute | solution.py:24
  10.3 2.8 %collective-permute-start.1 = (s32[2]{0:T(128)S(1)}, s32[2]{0:T(128)S(1)}, u32[]{:S(2)}, u32[]{:S(2)}) collective-permute-start(s32[2]{0:T(128)S(1)} %get-tuple-element.16), channel_id=1, source_target_pairs={{0,112},{16,0},{32,16},{48,32},{64,48},{80,64},{96,80},{112,96},{1... | collective-permute-start | bytes 32 | tf_op jit(solution)/shard_map/ppermute | solution.py:24
  13.1 0.0 copy-start
  13.8 0.0 copy-done
  13.8 0.1 fusion.6
  13.9 0.1 pad_maximum_fusion.1
  14.0 0.1 dynamic_slice.3
  14.0 0.1 broadcast_in_dim.9
  14.1 0.1 copy.7
  14.2 0.1 collective-permute-done
  14.3 0.0 collective-permute-done.1
  14.4 0.1 broadcast_compare_fusion
  14.4 6.4 %all-to-all-done = f32[16,4,16,128]{3,2,1,0:T(8,128)S(1)} async-done(((f32[16,4,16,128]{3,2,1,0:T(8,128)}), f32[16,4,16,128]{3,2,1,0:T(8,128)S(1)}, u32[]{:S(2)}, u32[]{:S(2)}) %all-to-all-start) | async-done | bytes 524320 | tf_op jit(solution)/shard_map/all_to_all | solution.py:422
  20.9 3.0 %collective-permute-start.3 = (f32[16,4,2,128]{3,2,1,0:T(2,128)S(1)}, f32[16,4,2,128]{3,2,1,0:T(2,128)S(1)}, u32[]{:S(2)}, u32[]{:S(2)}) collective-permute-start(f32[16,4,2,128]{3,2,1,0:T(2,128)S(1)} %get-tuple-element.11), channel_id=1, source_target_pairs={{0,112},{16,0},{32,16},{48,32},{64,48},{80,64},{96,80},{112,96},{1... | collective-permute-start | bytes 196616 | tf_op jit(solution)/shard_map/ppermute | solution.py:24
  23.9 0.0 collective-permute-start.2
  23.9 0.1 add_select_fusion.shift_tiles
  24.0 3.0 %turn_own.1 = (f32[16,88,128]{2,1,0:T(8,128)}, f32[8,16,128]{2,1,0:T(8,128)S(1)}) custom-call(s32[16]{0:T(128)S(1)} %and_select_fusion.shifts, f32[16,64,128]{2,1,0:T(8,128)S(1)} %bitcast.22), custom_call_target="tpu_custom_call" | custom-call | flops 4000000 | bytes 4000000 | tf_op jit(solution)/shard_map/turn_own/pallas_call | solution.py:438
  27.0 0.0 collective-permute-done.3
  27.0 2.1 %collective-permute-done.2 = f32[16,4,2,128]{3,2,1,0:T(2,128)S(1)} collective-permute-done((f32[16,4,2,128]{3,2,1,0:T(2,128)S(1)}, f32[16,4,2,128]{3,2,1,0:T(2,128)S(1)}, u32[]{:S(2)}, u32[]{:S(2)}) %collective-permute-start.2) | collective-permute-done | bytes 65568 | tf_op jit(solution)/shard_map/ppermute | solution.py:24
  29.1 0.9 %turn_ghost.1 = f32[16,88,128]{2,1,0:T(8,128)} custom-call(s32[4,128]{1,0:T(4,128)S(1)} %add_select_fusion.shift_tiles, f32[16,8,128]{2,1,0:T(8,128)S(1)} %bitcast.24, f32[16,8,128]{2,1,0:T(8,128)S(1)} %bitcast.23, f32[8,16,128]{2,1,0:T(8,128)S(1)} %get-tuple-element.7.strips_in, f32[16,88,128]{2,1,0:T(8,128)} %get-tuple-element.8.chunk), custom_call_target="tpu_custom_call", output_to_operand_aliasing={{}: (4, {})} | custom-call | tf_op jit(solution)/shard_map/turn_ghost/pallas_call | solution.py:441
  30.0 5.9 %all-to-all-start.1 = ((f32[16,88,128]{2,1,0:T(8,128)}), f32[16,88,128]{2,1,0:T(8,128)S(1)}, u32[]{:S(2)}, u32[]{:S(2)}) async-start(f32[16,88,128]{2,1,0:T(8,128)} %turn_ghost.1), calls=%async_computation.1 | async-start | bytes 1441792 | tf_op jit(solution)/shard_map/all_to_all | solution.py:448
  35.9 0.1 broadcast_bitcast_fusion
  36.0 0.1 reshape.31
  36.1 0.1 slice_bitcast_fusion.2
  36.2 0.1 maximum_bitcast_fusion
  36.2 0.1 pad_maximum_fusion
  36.3 13.4 %all-to-all-done.1 = f32[16,88,128]{2,1,0:T(8,128)S(1)} async-done(((f32[16,88,128]{2,1,0:T(8,128)}), f32[16,88,128]{2,1,0:T(8,128)S(1)}, u32[]{:S(2)}, u32[]{:S(2)}) %all-to-all-start.1) | async-done | bytes 720928 | tf_op jit(solution)/shard_map/all_to_all | solution.py:448
  49.8 3.4 %two_sections.1 = f32[64,16,128]{2,1,0:T(8,128)} custom-call(f32[24,8,128]{2,1,0:T(8,128)S(1)} %broadcast_in_dim.11.drift_rows, f32[1408,128]{1,0:T(8,128)S(1)} %bitcast.21), custom_call_target="tpu_custom_call" | custom-call | tf_op jit(solution)/shard_map/two_sections/pallas_call | solution.py:451
  (9 shorter events, 0.1 us)
Async XLA Ops:
  0.0 9.4 %copy-start.1 = (s32[16]{0:T(128)S(1)}, s32[16]{0:T(128)}, u32[]{:S(2)}) copy-start(s32[16]{0:T(128)} %param.6) | copy-start | bytes 196
  0.0 20.8 %all-to-all-start = ((f32[16,4,16,128]{3,2,1,0:T(8,128)}), f32[16,4,16,128]{3,2,1,0:T(8,128)S(1)}, u32[]{:S(2)}, u32[]{:S(2)}) async-start(f32[16,4,16,128]{3,2,1,0:T(8,128)} %bitcast.25), calls=%async_computation | async-start | bytes 1048576 | tf_op jit(solution)/shard_map/all_to_all | solution.py:422
  9.5 4.8 %collective-permute-start = (s32[2]{0:T(128)S(1)}, s32[2]{0:T(128)S(1)}, u32[]{:S(2)}, u32[]{:S(2)}) collective-permute-start(s32[2]{0:T(128)S(1)} %get-tuple-element.15), channel_id=1, source_target_pairs={{0,16},{16,32},{32,48},{48,64},{64,80},{80,96},{96,112},{112,0},{1... | collective-permute-start | bytes 32 | tf_op jit(solution)/shard_map/ppermute | solution.py:24
  10.3 4.1 %collective-permute-start.1 = (s32[2]{0:T(128)S(1)}, s32[2]{0:T(128)S(1)}, u32[]{:S(2)}, u32[]{:S(2)}) collective-permute-start(s32[2]{0:T(128)S(1)} %get-tuple-element.16), channel_id=1, source_target_pairs={{0,112},{16,0},{32,16},{48,32},{64,48},{80,64},{96,80},{112,96},{1... | collective-permute-start | bytes 32 | tf_op jit(solution)/shard_map/ppermute | solution.py:24
  13.1 0.7 %copy-start = (f32[128]{0:T(128)S(1)}, f32[128]{0:T(128)}, u32[]{:S(2)}) copy-start(f32[128]{0:T(128)} %param.5) | copy-start | bytes 1540
  20.9 6.1 %collective-permute-start.3 = (f32[16,4,2,128]{3,2,1,0:T(2,128)S(1)}, f32[16,4,2,128]{3,2,1,0:T(2,128)S(1)}, u32[]{:S(2)}, u32[]{:S(2)}) collective-permute-start(f32[16,4,2,128]{3,2,1,0:T(2,128)S(1)} %get-tuple-element.11), channel_id=1, source_target_pairs={{0,112},{16,0},{32,16},{48,32},{64,48},{80,64},{96,80},{112,96},{1... | collective-permute-start | bytes 196616 | tf_op jit(solution)/shard_map/ppermute | solution.py:24
  23.9 5.2 %collective-permute-start.2 = (f32[16,4,2,128]{3,2,1,0:T(2,128)S(1)}, f32[16,4,2,128]{3,2,1,0:T(2,128)S(1)}, u32[]{:S(2)}, u32[]{:S(2)}) collective-permute-start(f32[16,4,2,128]{3,2,1,0:T(2,128)S(1)} %get-tuple-element.12), channel_id=1, source_target_pairs={{0,16},{16,32},{32,48},{48,64},{64,80},{80,96},{96,112},{112,0},{1... | collective-permute-start | bytes 196616 | tf_op jit(solution)/shard_map/ppermute | solution.py:24
  30.0 19.7 %all-to-all-start.1 = ((f32[16,88,128]{2,1,0:T(8,128)}), f32[16,88,128]{2,1,0:T(8,128)S(1)}, u32[]{:S(2)}, u32[]{:S(2)}) async-start(f32[16,88,128]{2,1,0:T(8,128)} %turn_ghost.1), calls=%async_computation.1 | async-start | bytes 1441792 | tf_op jit(solution)/shard_map/all_to_all | solution.py:448

commit v5 on v4

--- a/solution.py
+++ b/solution.py
@@ -178,21 +178,20 @@
     return pltpu.roll(tile, 1, 0)
 
 
-def low_side(here, residual):
-    vel_y = y_dn(here[2])
-    return y_dn(here[1]), vel_y + residual, y_dn(here[5]), vel_y
-
-
-def radial_edges(prev, here, drift_prev, drift, low_prev, low):
+def both_sides(row):
+    return [y_dn(field) for field in row], [y_up(field) for field in row]
+
+
+def radial_edges(prev, here, drift_prev, drift, left_prev, left):
     _, vel_x, _, vel_z, _, mag_x, mag_y, mag_z = here
     two_x = vel_x + prev[1]
     two_z = vel_z + prev[3]
     two_w = drift + drift_prev
-    four_x = two_x + (low[0] + low_prev[0])
-    four_w = two_w + (low[1] + low_prev[1])
+    four_x = two_x + (left[1] + left_prev[1])
+    four_w = two_w + ((left[2] + left_prev[2]) + ((drift - here[2]) + (drift_prev - prev[2])))
     mag_x_z = z_dn(mag_x)
-    emf_z = (0.125 * time_step) * (four_w * (mag_x + low[2]) - four_x * (mag_y + prev[6])) + (time_step * resist) * (
-        (mag_y - prev[6]) - (mag_x - low[2])
+    emf_z = (0.125 * time_step) * (four_w * (mag_x + left[5]) - four_x * (mag_y + prev[6])) + (time_step * resist) * (
+        (mag_y - prev[6]) - (mag_x - left[5])
     )
     emf_y = (0.125 * time_step) * (
         (two_x + z_dn(two_x)) * (mag_z + prev[7]) - (two_z + z_dn(two_z)) * (mag_x + mag_x_z)
@@ -200,41 +199,45 @@
     return emf_z, emf_y
 
 
-def row_step(prev, here, after, residual, low, low_after, edges, edges_after):
+def row_step(prev, here, after, residual, ahead_prev, sides, sides_after, edges, edges_after):
+    left, right = sides
+    left_after, right_after = sides_after
     log_rho, vel_x, vel_y, vel_z, entropy, mag_x, mag_y, mag_z = here
     drift = vel_y + residual
     half_x = (0.5 * time_step) * vel_x
     half_w = (0.5 * time_step) * drift
     half_z = (0.5 * time_step) * vel_z
 
-    def moved_by(index, left=None):
+    def moved_by(index):
         center = here[index]
         fore, back = after[index], prev[index]
-        left = y_dn(center) if left is None else left
-        right = y_up(center)
+        behind, ahead = left[index], right[index]
         under, over = z_dn(center), z_up(center)
-        d_x, d_y, d_z = fore - back, right - left, over - under
-        total = ((fore + back) + (left + right)) + (under + over)
+        d_x, d_y, d_z = fore - back, ahead - behind, over - under
+        total = ((fore + back) + (behind + ahead)) + (under + over)
         result = (time_step * viscous) * total + (1.0 - 6.0 * time_step * viscous) * center
         result = result - (half_x * d_x + half_w * d_y + half_z * d_z)
-        return result, d_x, d_y, d_z, left
-
-    next_l, l_x, l_y, l_z, _ = moved_by(0)
-    next_vx, vx_x, _, _, _ = moved_by(1, low[0])
-    next_vy, _, vy_y, _, _ = moved_by(2, low[3])
-    next_vz, _, _, vz_z, vz_left = moved_by(3)
-    next_s, s_x, s_y, s_z, _ = moved_by(4)
+        return result, d_x, d_y, d_z
+
+    next_l, l_x, l_y, l_z = moved_by(0)
+    next_vx, vx_x, _, _ = moved_by(1)
+    next_vy, _, vy_y, _ = moved_by(2)
+    next_vz, _, _, vz_z = moved_by(3)
+    next_s, s_x, s_y, s_z = moved_by(4)
 
     two_bx = mag_x + after[5]
-    two_by = mag_y + y_up(mag_y)
+    two_by = mag_y + right[6]
     two_bz = mag_z + z_up(mag_z)
-    two_bx_left = low[2] + low_after[2]
-    mag_z_y = y_dn(mag_z)
+    two_bx_left = left[5] + left_after[5]
+    mag_z_y = left[7]
     diff_y = after[6] - prev[6]
     diff_z = after[7] - prev[7]
-    cur_x = (y_up(two_bz) - (mag_z_y + z_up(mag_z_y))) - (z_up(two_by) - z_dn(two_by))
+    side_z = right[7] - mag_z_y
+    cur_x = (side_z + z_up(side_z)) - (z_up(two_by) - z_dn(two_by))
     cur_y = (z_up(two_bx) - z_dn(two_bx)) - (diff_z + z_up(diff_z))
-    cur_z = (diff_y + two_bx_left) + y_up(diff_y - two_bx)
+    cur_z = (diff_y + two_bx_left) + (
+        (right_after[6] - ahead_prev) - (right[5] + right_after[5])
+    )
     inverse = jnp.exp(-log_rho)
     eighth = (0.125 * time_step) * inverse
     next_l = next_l - (0.5 * time_step) * (vx_x + vy_y + vz_z)
@@ -259,21 +262,30 @@
 
     emf_z, emf_y = edges
     emf_z_after, emf_y_after = edges_after
-    pair_w = drift + low[1]
-    pair_z = vel_z + vz_left
+    pair_w = (drift + residual) + left[2]
+    pair_z = vel_z + left[3]
     mag_y_z = z_dn(mag_y)
     emf_x = (0.125 * time_step) * (
         (pair_z + z_dn(pair_z)) * (mag_y + mag_y_z) - (pair_w + z_dn(pair_w)) * (mag_z + mag_z_y)
     ) + (time_step * resist) * ((mag_z - mag_z_y) - (mag_y - mag_y_z))
-    next_bx = mag_x + (emf_z - y_up(emf_z)) + (z_up(emf_y) - emf_y)
+    next_bx = (mag_x + emf_z) + (z_up(emf_y) - emf_y)
     next_by = (
         mag_y
         + (emf_x - z_up(emf_x))
         + (emf_z_after - emf_z)
         - (0.25 * time_step * shear_rate * rotation) * (two_bx + two_bx_left)
     )
-    next_bz = mag_z + (emf_y - emf_y_after) + (y_up(emf_x) - emf_x)
-    return [next_l, next_vx, next_vy, next_vz, next_s, next_bx, next_by, next_bz]
+    next_bz = (mag_z - emf_x) + (emf_y - emf_y_after)
+    done = [next_l, next_vx, next_vy, next_vz, next_s, next_by]
+    return done, (next_bx, emf_z, next_bz, emf_x)
+
+
+DONE = (0, 1, 2, 3, 4, 6)
+
+
+def last_edges(pending):
+    next_bx, emf_z, next_bz, emf_x = pending
+    return next_bx - y_up(emf_z), next_bz + y_up(emf_x)
 
 
 def drift_tiles(drift, depth):
@@ -298,7 +310,7 @@
     chunk = own + 3 * ghost
     strip_at = wide
 
-    def kernel(drift_rows, source, out, moved, first, ends, evolved, sems):
+    def kernel(drift_rows, source, out, moved, first, whole, evolved, sems):
         flat_out = evolved.reshape(fields * depth * rows, LANES)
         lane = lax.broadcasted_iota(jnp.int32, (depth, LANES), 1)
 
@@ -332,60 +344,81 @@
         def row_of(ref, row):
             return [ref[field, row] for field in range(fields)]
 
-        def edges_of(ref, row):
+        def begin(ref, row):
             prev, here = row_of(ref, row - 1), row_of(ref, row)
-            drift_prev, drift = prev[2] + drift_rows[row - 1], here[2] + drift_rows[row]
-            low = low_side(here, drift_rows[row])
-            low_prev = low_side(prev, drift_rows[row - 1])
-            return low, radial_edges(prev, here, drift_prev, drift, low_prev, low)
+            sides_prev, sides = both_sides(prev), both_sides(here)
+            edges = radial_edges(
+                prev,
+                here,
+                prev[2] + drift_rows[row - 1],
+                here[2] + drift_rows[row],
+                sides_prev[0],
+                sides[0],
+            )
+            return sides_prev[1][6], sides, edges, (here[5], here[5], here[7], here[7])
 
         def step(ref, row, carried):
-            low, edges = carried
+            ahead_prev, sides, edges, _ = carried
             prev, here, after = row_of(ref, row - 1), row_of(ref, row), row_of(ref, row + 1)
             drift, drift_after = here[2] + drift_rows[row], after[2] + drift_rows[row + 1]
-            low_after = low_side(after, drift_rows[row + 1])
-            edges_after = radial_edges(here, after, drift, drift_after, low, low_after)
-            result = row_step(
-                prev, here, after, drift_rows[row], low, low_after, edges, edges_after
+            sides_after = both_sides(after)
+            edges_after = radial_edges(here, after, drift, drift_after, sides[0], sides_after[0])
+            done, pending = row_step(
+                prev, here, after, drift_rows[row], ahead_prev, sides, sides_after, edges, edges_after
             )
-            return result, (low_after, edges_after)
-
-        def first_row(row, edges):
-            result, edges = step(moved, row, edges)
-            for field in range(fields):
-                first[field, row] = result[field]
-            return edges
-
-        edges = edges_of(moved, strip_at + 1)
+            return done, (sides[1][6], sides_after, edges_after, pending)
+
+        def settle_first(row, carried):
+            first[5, row], first[7, row] = last_edges(carried[3])
+
+        def first_row(row, carried):
+            settle_first(row - 1, carried)
+            done, carried = step(moved, row, carried)
+            for field, value in zip(DONE, done):
+                first[field, row] = value
+            return carried
+
+        carried = begin(moved, strip_at + 1)
         for row in (strip_at + 1, strip_at + 2):
-            edges = first_row(row, edges)
+            carried = first_row(row, carried)
+        settle_first(strip_at + 2, carried)
         widen_strips(first)
-        lax.fori_loop(1, wide - 1, first_row, edges_of(moved, 1), unroll=6)
-
-        edges = edges_of(first, strip_at + 1)
-        for parity in range(2):
-            result, edges = step(first, strip_at + 1 + parity, edges)
-            for field in range(fields):
-                ends[field, parity] = 0.5 * (moved[field, strip_at + 1 + parity] + result[field])
-
-        def second_row(row, edges):
-            result, edges = step(first, row, edges)
-            place = row // 2
-            turn = (LANES - 3 * DEPTH - STRIP * place) % LANES
-            for field in range(fields):
-                whole = 0.5 * (moved[field, row] + result[field])
-                end = pltpu.roll(ends[field, row % 2], turn, 1)
-                flat_out[pl.ds(field * depth * rows + row - DEPTH, depth, stride=rows), :] = jnp.where(
-                    lane < LANES - 2 * DEPTH, pltpu.roll(whole, LANES - DEPTH, 1), end
-                )
-            return edges
-
-        edges = edges_of(first, DEPTH)
+        carried = lax.fori_loop(1, wide - 1, first_row, begin(moved, 1), unroll=wide - 2)
+        settle_first(wide - 2, carried)
+
+        def settle_second(row, carried):
+            for field, value in zip((5, 7), last_edges(carried[3])):
+                whole[field, row] = 0.5 * (moved[field, row] + value)
+
+        def second_row(row, carried):
+            settle_second(row - 1, carried)
+            done, carried = step(first, row, carried)
+            for field, value in zip(DONE, done):
+                whole[field, row] = 0.5 * (moved[field, row] + value)
+            return carried
+
+        carried = begin(first, strip_at + 1)
+        for row in (strip_at + 1, strip_at + 2):
+            carried = second_row(row, carried)
+        settle_second(strip_at + 2, carried)
+
+        carried = begin(first, DEPTH)
         copies = []
         for block in range(rows // TILE_ROWS):
             start = DEPTH + block * TILE_ROWS
-            edges = lax.fori_loop(start, start + TILE_ROWS, second_row, edges, unroll=4)
+            carried = lax.fori_loop(start, start + TILE_ROWS, second_row, carried, unroll=TILE_ROWS)
+            settle_second(start + TILE_ROWS - 1, carried)
             for field in range(fields):
+                for row in range(start, start + TILE_ROWS):
+                    turn = (LANES - 3 * DEPTH - STRIP * (row // 2)) % LANES
+                    end = pltpu.roll(whole[field, strip_at + 1 + row % 2], turn, 1)
+                    flat_out[pl.ds(field * depth * rows + row - DEPTH, depth, stride=rows), :] = (
+                        jnp.where(
+                            lane < LANES - 2 * DEPTH,
+                            pltpu.roll(whole[field, row], LANES - DEPTH, 1),
+                            end,
+                        )
+                    )
                 piece = (pl.ds(field * depth, depth), pl.ds(block * TILE_ROWS, TILE_ROWS))
                 copy = pltpu.make_async_copy(evolved.at[piece], out.at[piece], sems.at[block, field])
                 copy.start()
@@ -401,7 +434,7 @@
         scratch_shapes=[
             pltpu.VMEM((fields, wide + 4, depth, LANES), jnp.float32),
             pltpu.VMEM((fields, wide + 4, depth, LANES), jnp.float32),
-            pltpu.VMEM((fields, 2, depth, LANES), jnp.float32),
+            pltpu.VMEM((fields, wide + 4, depth, LANES), jnp.float32),
             pltpu.VMEM((fields * depth, rows, LANES), jnp.float32),
             pltpu.SemaphoreType.DMA((rows // TILE_ROWS, fields)),
         ],

time: 53.5 us -> 53 us (level)
  no operation moved by 1% of the time
where the time goes in v5:
time: 53 us; the launch traced here: 52.7 us
  waiting for transfers between devices  22.1 us (42%)
  starting transfers between devices  22 us (42%)
  Pallas kernels  6.9 us (13%)
  between operations  0.73 us (1%)
  local copies, waits for them, and re-layouts  0.69 us (1%)
    all_to_all x1, waiting for transfers between devices, local(): wide = lax.all_to_all(chunk, 'gy', split_axis=0, concat_axis=0, tiled=True)  13.4 us
    all_to_all x1, starting transfers between devices, local(): lax.all_to_all(state.reshape(groups, planes, rows, cols), 'gy', split_axi...  9.43 us
    ppermute x4, starting transfers between devices, passed_along(): return lax.ppermute(value, axis, pairs)  6.61 us
    all_to_all x1, waiting for transfers between devices, local(): lax.all_to_all(state.reshape(groups, planes, rows, cols), 'gy', split_axi...  6.39 us
    all_to_all x1, starting transfers between devices, local(): wide = lax.all_to_all(chunk, 'gy', split_axis=0, concat_axis=0, tiled=True)  5.91 us
    pallas_call x1, Pallas kernels, local(): turn_own(groups, rows, planes)  3.03 us
    pallas_call x1, Pallas kernels, local(): two_sections(fields, depth, rows)  2.95 us
    ppermute x4, waiting for transfers between devices, passed_along(): return lax.ppermute(value, axis, pairs)  2.23 us
  transfers between devices with their start and end apart: 6, of which 4 were waited for; matrix products, arithmetic and copies ran while one was open for 2% of the time, Pallas kernels for 6%

profile of v5, /device:TPU:1, one launch (start us, length us, event | category | flops | bytes accessed | tf_op | source)
XLA Modules:
  0.0 52.7 jit_solution(17826724505707278979)
XLA Ops:
  0.0 0.0 copy-start.1
  0.0 9.4 %all-to-all-start = ((f32[16,4,16,128]{3,2,1,0:T(8,128)}), f32[16,4,16,128]{3,2,1,0:T(8,128)S(1)}, u32[]{:S(2)}, u32[]{:S(2)}) async-start(f32[16,4,16,128]{3,2,1,0:T(8,128)} %bitcast.25), calls=%async_computation | async-start | bytes 1048576 | tf_op jit(solution)/shard_map/all_to_all | solution.py:455
  9.4 0.0 copy-done.1
  9.4 0.1 fusion.5
  9.5 0.8 %collective-permute-start = (s32[2]{0:T(128)S(1)}, s32[2]{0:T(128)S(1)}, u32[]{:S(2)}, u32[]{:S(2)}) collective-permute-start(s32[2]{0:T(128)S(1)} %get-tuple-element.15), channel_id=1, source_target_pairs={{0,16},{16,32},{32,48},{48,64},{64,80},{80,96},{96,112},{112,0},{1... | collective-permute-start | bytes 32 | tf_op jit(solution)/shard_map/ppermute | solution.py:24
  10.3 2.8 %collective-permute-start.1 = (s32[2]{0:T(128)S(1)}, s32[2]{0:T(128)S(1)}, u32[]{:S(2)}, u32[]{:S(2)}) collective-permute-start(s32[2]{0:T(128)S(1)} %get-tuple-element.16), channel_id=1, source_target_pairs={{0,112},{16,0},{32,16},{48,32},{64,48},{80,64},{96,80},{112,96},{1... | collective-permute-start | bytes 32 | tf_op jit(solution)/shard_map/ppermute | solution.py:24
  13.1 0.0 copy-start
  13.8 0.0 copy-done
  13.8 0.1 fusion.6
  13.9 0.1 pad_maximum_fusion.1
  14.0 0.1 dynamic_slice.3
  14.0 0.1 broadcast_in_dim.9
  14.1 0.1 copy.7
  14.2 0.1 collective-permute-done
  14.3 0.0 collective-permute-done.1
  14.4 0.1 broadcast_compare_fusion
  14.4 6.4 %all-to-all-done = f32[16,4,16,128]{3,2,1,0:T(8,128)S(1)} async-done(((f32[16,4,16,128]{3,2,1,0:T(8,128)}), f32[16,4,16,128]{3,2,1,0:T(8,128)S(1)}, u32[]{:S(2)}, u32[]{:S(2)}) %all-to-all-start) | async-done | bytes 524320 | tf_op jit(solution)/shard_map/all_to_all | solution.py:455
  20.9 3.0 %collective-permute-start.3 = (f32[16,4,2,128]{3,2,1,0:T(2,128)S(1)}, f32[16,4,2,128]{3,2,1,0:T(2,128)S(1)}, u32[]{:S(2)}, u32[]{:S(2)}) collective-permute-start(f32[16,4,2,128]{3,2,1,0:T(2,128)S(1)} %get-tuple-element.11), channel_id=1, source_target_pairs={{0,112},{16,0},{32,16},{48,32},{64,48},{80,64},{96,80},{112,96},{1... | collective-permute-start | bytes 196616 | tf_op jit(solution)/shard_map/ppermute | solution.py:24
  23.9 0.0 collective-permute-start.2
  23.9 0.1 add_select_fusion.shift_tiles
  24.0 3.0 %turn_own.1 = (f32[16,88,128]{2,1,0:T(8,128)}, f32[8,16,128]{2,1,0:T(8,128)S(1)}) custom-call(s32[16]{0:T(128)S(1)} %and_select_fusion.shifts, f32[16,64,128]{2,1,0:T(8,128)S(1)} %bitcast.22), custom_call_target="tpu_custom_call" | custom-call | flops 4000000 | bytes 4000000 | tf_op jit(solution)/shard_map/turn_own/pallas_call | solution.py:471
  27.0 0.0 collective-permute-done.3
  27.0 2.1 %collective-permute-done.2 = f32[16,4,2,128]{3,2,1,0:T(2,128)S(1)} collective-permute-done((f32[16,4,2,128]{3,2,1,0:T(2,128)S(1)}, f32[16,4,2,128]{3,2,1,0:T(2,128)S(1)}, u32[]{:S(2)}, u32[]{:S(2)}) %collective-permute-start.2) | collective-permute-done | bytes 65568 | tf_op jit(solution)/shard_map/ppermute | solution.py:24
  29.1 0.9 %turn_ghost.1 = f32[16,88,128]{2,1,0:T(8,128)} custom-call(s32[4,128]{1,0:T(4,128)S(1)} %add_select_fusion.shift_tiles, f32[16,8,128]{2,1,0:T(8,128)S(1)} %bitcast.24, f32[16,8,128]{2,1,0:T(8,128)S(1)} %bitcast.23, f32[8,16,128]{2,1,0:T(8,128)S(1)} %get-tuple-element.7.strips_in, f32[16,88,128]{2,1,0:T(8,128)} %get-tuple-element.8.chunk), custom_call_target="tpu_custom_call", output_to_operand_aliasing={{}: (4, {})} | custom-call | tf_op jit(solution)/shard_map/turn_ghost/pallas_call | solution.py:474
  30.0 5.9 %all-to-all-start.1 = ((f32[16,88,128]{2,1,0:T(8,128)}), f32[16,88,128]{2,1,0:T(8,128)S(1)}, u32[]{:S(2)}, u32[]{:S(2)}) async-start(f32[16,88,128]{2,1,0:T(8,128)} %turn_ghost.1), calls=%async_computation.1 | async-start | bytes 1441792 | tf_op jit(solution)/shard_map/all_to_all | solution.py:481
  35.9 0.1 broadcast_bitcast_fusion
  36.0 0.1 reshape.31
  36.1 0.1 slice_bitcast_fusion.2
  36.2 0.1 maximum_bitcast_fusion
  36.2 0.1 pad_maximum_fusion
  36.3 13.4 %all-to-all-done.1 = f32[16,88,128]{2,1,0:T(8,128)S(1)} async-done(((f32[16,88,128]{2,1,0:T(8,128)}), f32[16,88,128]{2,1,0:T(8,128)S(1)}, u32[]{:S(2)}, u32[]{:S(2)}) %all-to-all-start.1) | async-done | bytes 720928 | tf_op jit(solution)/shard_map/all_to_all | solution.py:481
  49.8 3.0 %two_sections.1 = f32[64,16,128]{2,1,0:T(8,128)} custom-call(f32[24,8,128]{2,1,0:T(8,128)S(1)} %broadcast_in_dim.11.drift_rows, f32[1408,128]{1,0:T(8,128)S(1)} %bitcast.21), custom_call_target="tpu_custom_call" | custom-call | tf_op jit(solution)/shard_map/two_sections/pallas_call | solution.py:484
  (9 shorter events, 0.1 us)
Async XLA Ops:
  0.0 9.4 %copy-start.1 = (s32[16]{0:T(128)S(1)}, s32[16]{0:T(128)}, u32[]{:S(2)}) copy-start(s32[16]{0:T(128)} %param.6) | copy-start | bytes 196
  0.0 20.8 %all-to-all-start = ((f32[16,4,16,128]{3,2,1,0:T(8,128)}), f32[16,4,16,128]{3,2,1,0:T(8,128)S(1)}, u32[]{:S(2)}, u32[]{:S(2)}) async-start(f32[16,4,16,128]{3,2,1,0:T(8,128)} %bitcast.25), calls=%async_computation | async-start | bytes 1048576 | tf_op jit(solution)/shard_map/all_to_all | solution.py:455
  9.5 4.8 %collective-permute-start = (s32[2]{0:T(128)S(1)}, s32[2]{0:T(128)S(1)}, u32[]{:S(2)}, u32[]{:S(2)}) collective-permute-start(s32[2]{0:T(128)S(1)} %get-tuple-element.15), channel_id=1, source_target_pairs={{0,16},{16,32},{32,48},{48,64},{64,80},{80,96},{96,112},{112,0},{1... | collective-permute-start | bytes 32 | tf_op jit(solution)/shard_map/ppermute | solution.py:24
  10.3 4.1 %collective-permute-start.1 = (s32[2]{0:T(128)S(1)}, s32[2]{0:T(128)S(1)}, u32[]{:S(2)}, u32[]{:S(2)}) collective-permute-start(s32[2]{0:T(128)S(1)} %get-tuple-element.16), channel_id=1, source_target_pairs={{0,112},{16,0},{32,16},{48,32},{64,48},{80,64},{96,80},{112,96},{1... | collective-permute-start | bytes 32 | tf_op jit(solution)/shard_map/ppermute | solution.py:24
  13.1 0.7 %copy-start = (f32[128]{0:T(128)S(1)}, f32[128]{0:T(128)}, u32[]{:S(2)}) copy-start(f32[128]{0:T(128)} %param.5) | copy-start | bytes 1540
  20.9 6.1 %collective-permute-start.3 = (f32[16,4,2,128]{3,2,1,0:T(2,128)S(1)}, f32[16,4,2,128]{3,2,1,0:T(2,128)S(1)}, u32[]{:S(2)}, u32[]{:S(2)}) collective-permute-start(f32[16,4,2,128]{3,2,1,0:T(2,128)S(1)} %get-tuple-element.11), channel_id=1, source_target_pairs={{0,112},{16,0},{32,16},{48,32},{64,48},{80,64},{96,80},{112,96},{1... | collective-permute-start | bytes 196616 | tf_op jit(solution)/shard_map/ppermute | solution.py:24
  23.9 5.2 %collective-permute-start.2 = (f32[16,4,2,128]{3,2,1,0:T(2,128)S(1)}, f32[16,4,2,128]{3,2,1,0:T(2,128)S(1)}, u32[]{:S(2)}, u32[]{:S(2)}) collective-permute-start(f32[16,4,2,128]{3,2,1,0:T(2,128)S(1)} %get-tuple-element.12), channel_id=1, source_target_pairs={{0,16},{16,32},{32,48},{48,64},{64,80},{80,96},{96,112},{112,0},{1... | collective-permute-start | bytes 196616 | tf_op jit(solution)/shard_map/ppermute | solution.py:24
  30.0 19.7 %all-to-all-start.1 = ((f32[16,88,128]{2,1,0:T(8,128)}), f32[16,88,128]{2,1,0:T(8,128)S(1)}, u32[]{:S(2)}, u32[]{:S(2)}) async-start(f32[16,88,128]{2,1,0:T(8,128)} %turn_ghost.1), calls=%async_computation.1 | async-start | bytes 1441792 | tf_op jit(solution)/shard_map/all_to_all | solution.py:481

commit v6 on v5

--- a/solution.py
+++ b/solution.py
@@ -14,6 +14,7 @@
 
 LANES = 128
 TILE_ROWS = 8
+FIRST = 1
 DEPTH = 2
 STRIP = 4 * DEPTH
 
@@ -98,67 +99,71 @@
     )
 
 
-def turn_ghost(groups, rows, planes):
+def turn_ghost(groups, rows, planes, side, last):
     own = rows * planes
     ghost = DEPTH * planes
-    zone = 3 * ghost
-
-    def kernel(shift_tiles, low, high, strips_in, chunk, out, lines, windows, sems):
-        shift_rows = shift_tiles[...]
-        amounts = [shift_rows[entry, 0] for entry in range(2 * DEPTH)]
-        lay_twice(low, lines, 0, ghost, groups)
-        lay_twice(high, lines, ghost, ghost, groups)
-        flat = lines.reshape((2 * groups + 1) * 2 * ghost, LANES)
-        target = windows.reshape(3 * groups * ghost, LANES)
+
+    def kernel(source, strips_in, chunk, out, *rest):
+        if last:
+            lines, windows, sems = rest
+        else:
+            strips_out, lines, windows, sems = rest
+        shift_rows = source[groups]
+        amounts = [shift_rows[entry, 0].astype(jnp.int32) for entry in range(DEPTH)]
+        lay_twice(source, lines, 0, ghost, groups)
+        flat = lines.reshape((2 * groups + 1) * ghost, LANES)
+        target = windows.reshape(2 * groups * ghost, LANES)
         lane = lax.broadcasted_iota(jnp.int32, (groups, LANES), 1)
         strips = [
             [strips_in[plane * 2 + parity] for plane in range(planes)] for parity in range(2)
         ]
 
-        def leave(part):
+        def leave(slot, part):
             copy = pltpu.make_async_copy(
-                windows.at[part], out.at[:, pl.ds(own + part * ghost, ghost)], sems.at[part]
+                windows.at[slot], out.at[:, pl.ds(own + part * ghost, ghost)], sems.at[slot]
             )
             copy.start()
             return copy
 
-        copies = []
-        for side in range(2):
-            for row in range(DEPTH):
-                wide_row = row + side * (rows + DEPTH)
-                for plane in range(planes):
-                    line = side * ghost + plane * DEPTH + row
-                    window, rim, part = turned_line(
-                        flat, line, 2 * ghost, groups, amounts[side * DEPTH + row], lane
-                    )
-                    place = side * groups * ghost + plane * DEPTH + row
-                    target[pl.ds(place, groups, stride=ghost), :] = window
-                    strips[wide_row % 2][plane] = placed_strip(
-                        rim, part, wide_row // 2, lane, strips[wide_row % 2][plane]
-                    )
-            copies.append(leave(side))
+        for row in range(DEPTH):
+            wide_row = row + side * (rows + DEPTH)
+            for plane in range(planes):
+                place = plane * DEPTH + row
+                window, rim, part = turned_line(flat, place, ghost, groups, amounts[row], lane)
+                target[pl.ds(place, groups, stride=ghost), :] = window
+                strips[wide_row % 2][plane] = placed_strip(
+                    rim, part, wide_row // 2, lane, strips[wide_row % 2][plane]
+                )
+        copies = [leave(0, side)]
         for plane in range(planes):
             for parity in range(2):
-                place = 2 * groups * ghost + plane * DEPTH + parity
-                target[pl.ds(place, groups, stride=ghost), :] = strips[parity][plane]
-        copies.append(leave(2))
+                if last:
+                    place = groups * ghost + plane * DEPTH + parity
+                    target[pl.ds(place, groups, stride=ghost), :] = strips[parity][plane]
+                else:
+                    strips_out[plane * 2 + parity] = strips[parity][plane]
+        if last:
+            copies.append(leave(1, 2))
         for copy in copies:
             copy.wait()
 
+    chunk_shape = jax.ShapeDtypeStruct((groups, own + 3 * ghost, LANES), jnp.float32)
+    strip_shape = jax.ShapeDtypeStruct((2 * planes, groups, LANES), jnp.float32)
     return pl.pallas_call(
         kernel,
-        in_specs=[pl.BlockSpec(memory_space=pltpu.VMEM)] * 4
+        in_specs=[pl.BlockSpec(memory_space=pltpu.VMEM)] * 2
         + [pl.BlockSpec(memory_space=pl.ANY)],
-        out_shape=jax.ShapeDtypeStruct((groups, own + zone, LANES), jnp.float32),
-        out_specs=pl.BlockSpec(memory_space=pl.ANY),
-        input_output_aliases={4: 0},
+        out_shape=(chunk_shape,) if last else (chunk_shape, strip_shape),
+        out_specs=(pl.BlockSpec(memory_space=pl.ANY),)
+        + (() if last else (pl.BlockSpec(memory_space=pltpu.VMEM),)),
+        input_output_aliases={2: 0},
         scratch_shapes=[
-            pltpu.VMEM((2 * groups + 1, 2 * ghost, LANES), jnp.float32),
-            pltpu.VMEM((3, groups, ghost, LANES), jnp.float32),
-            pltpu.SemaphoreType.DMA((3,)),
+            pltpu.VMEM((2 * groups + 1, ghost, LANES), jnp.float32),
+            pltpu.VMEM((2, groups, ghost, LANES), jnp.float32),
+            pltpu.SemaphoreType.DMA((2,)),
         ],
         compiler_params=pltpu.CompilerParams(vmem_limit_bytes=24 * 1024 * 1024),
-        name="turn_ghost",
+        name="turn_last_side" if last else "turn_first_side",
     )
 
 
@@ -455,28 +460,30 @@
     lines = lax.all_to_all(
         state.reshape(groups, planes, rows, cols), "gy", split_axis=0, concat_axis=0, tiled=True
     )
-    low = passed_along(lines[:, :, rows - DEPTH :], "gx", 1)
-    high = passed_along(lines[:, :, :DEPTH], "gx", -1)
-    low_shift = passed_along(shift_rows[rows - DEPTH :], "gx", 1)
-    high_shift = passed_along(shift_rows[:DEPTH], "gx", -1)
-    across = jnp.ones((1, cols), jnp.int32)
-    ghost_shifts = jnp.concatenate(
-        [
-            (low_shift - jnp.where(row_dev == 0, offset, 0))[:, None] * across,
-            (high_shift + jnp.where(row_dev == radial_count - 1, offset, 0))[:, None] * across,
-        ]
-    )
-    ghost_shifts = (ghost_shifts + DEPTH) % cells_y
+
+    def with_shifts(part, shifts):
+        shifts = ((shifts + DEPTH) % cells_y).astype(jnp.float32)
+        extra = jnp.broadcast_to(shifts[None, None, :, None], (1, planes, DEPTH, cols))
+        return jnp.concatenate([part, extra])
+
+    up = jnp.where(row_dev == radial_count - 1, offset, 0)
+    down = jnp.where(row_dev == 0, offset, 0)
+    low = with_shifts(lines[:, :, rows - DEPTH :], shift_rows[rows - DEPTH :] - up)
+    high = with_shifts(lines[:, :, :DEPTH], shift_rows[:DEPTH] + down)
+    low, high = passed_along(low, "gx", 1), passed_along(high, "gx", -1)
     own_shifts = shift_rows + DEPTH
     chunk, strips = turn_own(groups, rows, planes)(
         own_shifts % cells_y, lines.reshape(groups, planes * rows, cols)
     )
-    chunk = turn_ghost(groups, rows, planes)(
-        ghost_shifts,
-        low.reshape(groups, planes * DEPTH, cols),
-        high.reshape(groups, planes * DEPTH, cols),
-        strips,
-        chunk,
+    sides = (
+        low.reshape(groups + 1, planes * DEPTH, cols),
+        high.reshape(groups + 1, planes * DEPTH, cols),
+    )
+    chunk, strips = turn_ghost(groups, rows, planes, FIRST, False)(
+        sides[FIRST], strips, chunk
+    )
+    (chunk,) = turn_ghost(groups, rows, planes, 1 - FIRST, True)(
+        sides[1 - FIRST], strips, chunk
     )
     wide = lax.all_to_all(chunk, "gy", split_axis=0, concat_axis=0, tiled=True)
     padded = jnp.concatenate([residual[-DEPTH:], residual, residual[:DEPTH]])

time: 53 us -> 53.3 us (level)
  starting transfers between devices: 22 us -> 18.4 us
  waiting for transfers between devices: 22.1 us -> 24.4 us
  local copies, waits for them, and re-layouts: 0.69 us -> 1.41 us
  Pallas kernels: 6.9 us -> 7.58 us
    ppermute x4 -> x2, starting transfers between devices: 6.61 us -> 3.08 us  [passed_along(): return lax.ppermute(value, axis, pairs)]
    all_to_all x1, waiting for transfers between devices: 6.39 us -> 9.9 us  [local(): lax.all_to_all(state.reshape(groups, planes, rows, cols), 'gy', split_axi...]
    ppermute x4 -> x2, waiting for transfers between devices: 2.23 us -> 1.1 us  [passed_along(): return lax.ppermute(value, axis, pairs)]
    pallas_call x1 -> x2, Pallas kernels: 0.91 us -> 1.63 us  [the longest x1 0.83 us: local(): turn_ghost(groups, rows, planes, 1 - FIRST, True)]
    unnamed x4, local copies, waits for them, and re-layouts: 0.01 us -> 0.65 us
  transfers between devices with their start and end apart: 6 -> 4, of which waited for: 4 -> 3; matrix products, arithmetic and copies ran while one was open for 2% -> 2% of each run, Pallas kernels for 6% -> 7%
where the time goes in v6:
time: 53.3 us; the launch traced here: 53 us
  waiting for transfers between devices  24.4 us (46%)
  starting transfers between devices  18.4 us (35%)
  Pallas kernels  7.58 us (14%)
  local copies, waits for them, and re-layouts  1.41 us (3%)
  between operations  0.75 us (1%)
    all_to_all x1, waiting for transfers between devices, local(): wide = lax.all_to_all(chunk, 'gy', split_axis=0, concat_axis=0, tiled=True)  13.4 us
    all_to_all x1, waiting for transfers between devices, local(): lax.all_to_all(state.reshape(groups, planes, rows, cols), 'gy', split_axi...  9.9 us
    all_to_all x1, starting transfers between devices, local(): lax.all_to_all(state.reshape(groups, planes, rows, cols), 'gy', split_axi...  9.43 us
    all_to_all x1, starting transfers between devices, local(): wide = lax.all_to_all(chunk, 'gy', split_axis=0, concat_axis=0, tiled=True)  5.91 us
    ppermute x2, starting transfers between devices, passed_along(): return lax.ppermute(value, axis, pairs)  3.08 us
    pallas_call x1, Pallas kernels, local(): turn_own(groups, rows, planes)  3 us
    pallas_call x1, Pallas kernels, local(): two_sections(fields, depth, rows)  2.95 us
    ppermute x2, waiting for transfers between devices, passed_along(): return lax.ppermute(value, axis, pairs)  1.1 us
  transfers between devices with their start and end apart: 4, of which 3 were waited for; matrix products, arithmetic and copies ran while one was open for 2% of the time, Pallas kernels for 7%

profile of v6, /device:TPU:1, one launch (start us, length us, event | category | flops | bytes accessed | tf_op | source)
XLA Modules:
  0.0 53.0 jit_solution(9816267846904945493)
XLA Ops:
  0.0 0.0 copy-start.1
  0.0 9.4 %all-to-all-start = ((f32[16,4,16,128]{3,2,1,0:T(8,128)}), f32[16,4,16,128]{3,2,1,0:T(8,128)S(1)}, u32[]{:S(2)}, u32[]{:S(2)}) async-start(f32[16,4,16,128]{3,2,1,0:T(8,128)} %bitcast.25), calls=%async_computation | async-start | bytes 1048576 | tf_op jit(solution)/shard_map/all_to_all | solution.py:460
  9.4 0.0 copy-done.1
  10.1 0.0 copy-start
  10.1 0.6 %copy-done = f32[128]{0:T(128)S(1)} copy-done((f32[128]{0:T(128)S(1)}, f32[128]{0:T(128)}, u32[]{:S(2)}) %copy-start) | copy-done | bytes 536
  10.8 0.1 fusion.6
  10.8 0.1 fusion.1
  10.9 9.9 %all-to-all-done = f32[16,4,16,128]{3,2,1,0:T(8,128)S(1)} async-done(((f32[16,4,16,128]{3,2,1,0:T(8,128)}), f32[16,4,16,128]{3,2,1,0:T(8,128)S(1)}, u32[]{:S(2)}, u32[]{:S(2)}) %all-to-all-start) | async-done | bytes 524320 | tf_op jit(solution)/shard_map/all_to_all | solution.py:460
  20.9 0.1 broadcast_in_dim.17
  21.0 3.0 %collective-permute-start.1 = (f32[17,4,2,128]{3,2,1,0:T(2,128)S(1)}, f32[17,4,2,128]{3,2,1,0:T(2,128)S(1)}, u32[]{:S(2)}, u32[]{:S(2)}) collective-permute-start(f32[17,4,2,128]{3,2,1,0:T(2,128)S(1)} %pad_maximum_fusion.1), channel_id=1, source_target_pairs={{0,112},{16,0},{32,16},{48,32},{64,48},{80,64},{96,80},{112,96},{1... | collective-permute-start | bytes 208904 | tf_op jit(solution)/shard_map/ppermute | solution.py:25
  24.0 0.1 broadcast_in_dim.16
  24.1 0.1 collective-permute-start
  24.2 0.1 pad_maximum_fusion.3
  24.3 0.1 dynamic_slice.3
  24.3 0.1 broadcast_in_dim.13
  24.4 0.1 copy.8
  24.5 3.0 %turn_own.1 = (f32[16,88,128]{2,1,0:T(8,128)}, f32[8,16,128]{2,1,0:T(8,128)S(1)}) custom-call(s32[16]{0:T(128)S(1)} %and_select_fusion.shifts, f32[16,64,128]{2,1,0:T(8,128)S(1)} %bitcast.22), custom_call_target="tpu_custom_call" | custom-call | flops 4000000 | bytes 4000000 | tf_op jit(solution)/shard_map/turn_own/pallas_call | solution.py:475
  27.5 0.0 collective-permute-done.1
  27.5 0.8 %turn_first_side.1 = (f32[16,88,128]{2,1,0:T(8,128)}, f32[8,16,128]{2,1,0:T(8,128)S(1)}) custom-call(f32[17,8,128]{2,1,0:T(8,128)S(1)} %bitcast.24, f32[8,16,128]{2,1,0:T(8,128)S(1)} %get-tuple-element.9.strips_in, f32[16,88,128]{2,1,0:T(8,128)} %get-tuple-element.10.chunk), custom_call_target="tpu_custom_call", output_to_operand_aliasing={{0}: (2, {})} | custom-call | tf_op jit(solution)/shard_map/turn_first_side/pallas_call | solution.py:482
  28.3 1.1 %collective-permute-done = f32[17,4,2,128]{3,2,1,0:T(2,128)S(1)} collective-permute-done((f32[17,4,2,128]{3,2,1,0:T(2,128)S(1)}, f32[17,4,2,128]{3,2,1,0:T(2,128)S(1)}, u32[]{:S(2)}, u32[]{:S(2)}) %collective-permute-start) | collective-permute-done | bytes 69664 | tf_op jit(solution)/shard_map/ppermute | solution.py:25
  29.4 0.8 %turn_last_side.1 = f32[16,88,128]{2,1,0:T(8,128)} custom-call(f32[17,8,128]{2,1,0:T(8,128)S(1)} %bitcast.23, f32[8,16,128]{2,1,0:T(8,128)S(1)} %get-tuple-element.11.strips_in, f32[16,88,128]{2,1,0:T(8,128)} %get-tuple-element.12.chunk), custom_call_target="tpu_custom_call", output_to_operand_aliasing={{}: (2, {})} | custom-call | tf_op jit(solution)/shard_map/turn_last_side/pallas_call | solution.py:485
  30.3 5.9 %all-to-all-start.1 = ((f32[16,88,128]{2,1,0:T(8,128)}), f32[16,88,128]{2,1,0:T(8,128)S(1)}, u32[]{:S(2)}, u32[]{:S(2)}) async-start(f32[16,88,128]{2,1,0:T(8,128)} %turn_last_side.1), calls=%async_computation.1 | async-start | bytes 1441792 | tf_op jit(solution)/shard_map/all_to_all | solution.py:488
  36.2 0.1 broadcast_bitcast_fusion
  36.2 0.1 reshape.35
  36.4 0.1 slice_bitcast_fusion.2
  36.4 0.1 maximum_bitcast_fusion
  36.5 0.1 pad_maximum_fusion.2
  36.6 13.4 %all-to-all-done.1 = f32[16,88,128]{2,1,0:T(8,128)S(1)} async-done(((f32[16,88,128]{2,1,0:T(8,128)}), f32[16,88,128]{2,1,0:T(8,128)S(1)}, u32[]{:S(2)}, u32[]{:S(2)}) %all-to-all-start.1) | async-done | bytes 720928 | tf_op jit(solution)/shard_map/all_to_all | solution.py:488
  50.0 3.0 %two_sections.1 = f32[64,16,128]{2,1,0:T(8,128)} custom-call(f32[24,8,128]{2,1,0:T(8,128)S(1)} %broadcast_in_dim.15.drift_rows, f32[1408,128]{1,0:T(8,128)S(1)} %bitcast.21), custom_call_target="tpu_custom_call" | custom-call | tf_op jit(solution)/shard_map/two_sections/pallas_call | solution.py:491
  (8 shorter events, 0.1 us)
Async XLA Ops:
  0.0 9.4 %copy-start.1 = (s32[16]{0:T(128)S(1)}, s32[16]{0:T(128)}, u32[]{:S(2)}) copy-start(s32[16]{0:T(128)} %param.6) | copy-start | bytes 196
  0.0 20.8 %all-to-all-start = ((f32[16,4,16,128]{3,2,1,0:T(8,128)}), f32[16,4,16,128]{3,2,1,0:T(8,128)S(1)}, u32[]{:S(2)}, u32[]{:S(2)}) async-start(f32[16,4,16,128]{3,2,1,0:T(8,128)} %bitcast.25), calls=%async_computation | async-start | bytes 1048576 | tf_op jit(solution)/shard_map/all_to_all | solution.py:460
  10.1 0.7 %copy-start = (f32[128]{0:T(128)S(1)}, f32[128]{0:T(128)}, u32[]{:S(2)}) copy-start(f32[128]{0:T(128)} %param.5) | copy-start | bytes 1540
  21.0 6.5 %collective-permute-start.1 = (f32[17,4,2,128]{3,2,1,0:T(2,128)S(1)}, f32[17,4,2,128]{3,2,1,0:T(2,128)S(1)}, u32[]{:S(2)}, u32[]{:S(2)}) collective-permute-start(f32[17,4,2,128]{3,2,1,0:T(2,128)S(1)} %pad_maximum_fusion.1), channel_id=1, source_target_pairs={{0,112},{16,0},{32,16},{48,32},{64,48},{80,64},{96,80},{112,96},{1... | collective-permute-start | bytes 208904 | tf_op jit(solution)/shard_map/ppermute | solution.py:25
  24.1 5.3 %collective-permute-start = (f32[17,4,2,128]{3,2,1,0:T(2,128)S(1)}, f32[17,4,2,128]{3,2,1,0:T(2,128)S(1)}, u32[]{:S(2)}, u32[]{:S(2)}) collective-permute-start(f32[17,4,2,128]{3,2,1,0:T(2,128)S(1)} %pad_maximum_fusion), channel_id=1, source_target_pairs={{0,16},{16,32},{32,48},{48,64},{64,80},{80,96},{96,112},{112,0},{1... | collective-permute-start | bytes 208904 | tf_op jit(solution)/shard_map/ppermute | solution.py:25
  30.3 19.7 %all-to-all-start.1 = ((f32[16,88,128]{2,1,0:T(8,128)}), f32[16,88,128]{2,1,0:T(8,128)S(1)}, u32[]{:S(2)}, u32[]{:S(2)}) async-start(f32[16,88,128]{2,1,0:T(8,128)} %turn_last_side.1), calls=%async_computation.1 | async-start | bytes 1441792 | tf_op jit(solution)/shard_map/all_to_all | solution.py:488

commit v7 on v5

--- a/solution.py
+++ b/solution.py
@@ -182,13 +182,13 @@
     return [y_dn(field) for field in row], [y_up(field) for field in row]
 
 
-def radial_edges(prev, here, drift_prev, drift, left_prev, left):
+def radial_edges(prev, here, residual_prev, residual, left_prev, left):
     _, vel_x, _, vel_z, _, mag_x, mag_y, mag_z = here
     two_x = vel_x + prev[1]
     two_z = vel_z + prev[3]
-    two_w = drift + drift_prev
+    two_w = (here[2] + residual) + (prev[2] + residual_prev)
     four_x = two_x + (left[1] + left_prev[1])
-    four_w = two_w + ((left[2] + left_prev[2]) + ((drift - here[2]) + (drift_prev - prev[2])))
+    four_w = two_w + ((left[2] + left_prev[2]) + (residual + residual_prev))
     mag_x_z = z_dn(mag_x)
     emf_z = (0.125 * time_step) * (four_w * (mag_x + left[5]) - four_x * (mag_y + prev[6])) + (time_step * resist) * (
         (mag_y - prev[6]) - (mag_x - left[5])
@@ -350,8 +350,8 @@
             edges = radial_edges(
                 prev,
                 here,
-                prev[2] + drift_rows[row - 1],
-                here[2] + drift_rows[row],
+                drift_rows[row - 1],
+                drift_rows[row],
                 sides_prev[0],
                 sides[0],
             )
@@ -360,7 +360,7 @@
         def step(ref, row, carried):
             ahead_prev, sides, edges, _ = carried
             prev, here, after = row_of(ref, row - 1), row_of(ref, row), row_of(ref, row + 1)
-            drift, drift_after = here[2] + drift_rows[row], after[2] + drift_rows[row + 1]
+            drift, drift_after = drift_rows[row], drift_rows[row + 1]
             sides_after = both_sides(after)
             edges_after = radial_edges(here, after, drift, drift_after, sides[0], sides_after[0])
             done, pending = row_step(

time: 53 us -> 53 us (level)
  no operation moved by 1% of the time
where the time goes in v7:
time: 53 us; the launch traced here: 52.7 us
  waiting for transfers between devices  22.1 us (42%)
  starting transfers between devices  22 us (42%)
  Pallas kernels  6.89 us (13%)
  between operations  0.73 us (1%)
  local copies, waits for them, and re-layouts  0.69 us (1%)
    all_to_all x1, waiting for transfers between devices, local(): wide = lax.all_to_all(chunk, 'gy', split_axis=0, concat_axis=0, tiled=True)  13.4 us
    all_to_all x1, starting transfers between devices, local(): lax.all_to_all(state.reshape(groups, planes, rows, cols), 'gy', split_axi...  9.43 us
    ppermute x4, starting transfers between devices, passed_along(): return lax.ppermute(value, axis, pairs)  6.61 us
    all_to_all x1, waiting for transfers between devices, local(): lax.all_to_all(state.reshape(groups, planes, rows, cols), 'gy', split_axi...  6.39 us
    all_to_all x1, starting transfers between devices, local(): wide = lax.all_to_all(chunk, 'gy', split_axis=0, concat_axis=0, tiled=True)  5.91 us
    pallas_call x1, Pallas kernels, local(): turn_own(groups, rows, planes)  3.03 us
    pallas_call x1, Pallas kernels, local(): two_sections(fields, depth, rows)  2.94 us
    ppermute x4, waiting for transfers between devices, passed_along(): return lax.ppermute(value, axis, pairs)  2.23 us
  transfers between devices with their start and end apart: 6, of which 4 were waited for; matrix products, arithmetic and copies ran while one was open for 2% of the time, Pallas kernels for 6%

profile of v7, /device:TPU:1, one launch (start us, length us, event | category | flops | bytes accessed | tf_op | source)
XLA Modules:
  0.0 52.7 jit_solution(3240599123437983399)
XLA Ops:
  0.0 0.0 copy-start.1
  0.0 9.4 %all-to-all-start = ((f32[16,4,16,128]{3,2,1,0:T(8,128)}), f32[16,4,16,128]{3,2,1,0:T(8,128)S(1)}, u32[]{:S(2)}, u32[]{:S(2)}) async-start(f32[16,4,16,128]{3,2,1,0:T(8,128)} %bitcast.25), calls=%async_computation | async-start | bytes 1048576 | tf_op jit(solution)/shard_map/all_to_all | solution.py:455
  9.4 0.0 copy-done.1
  9.4 0.1 fusion.5
  9.5 0.8 %collective-permute-start = (s32[2]{0:T(128)S(1)}, s32[2]{0:T(128)S(1)}, u32[]{:S(2)}, u32[]{:S(2)}) collective-permute-start(s32[2]{0:T(128)S(1)} %get-tuple-element.15), channel_id=1, source_target_pairs={{0,16},{16,32},{32,48},{48,64},{64,80},{80,96},{96,112},{112,0},{1... | collective-permute-start | bytes 32 | tf_op jit(solution)/shard_map/ppermute | solution.py:24
  10.3 2.8 %collective-permute-start.1 = (s32[2]{0:T(128)S(1)}, s32[2]{0:T(128)S(1)}, u32[]{:S(2)}, u32[]{:S(2)}) collective-permute-start(s32[2]{0:T(128)S(1)} %get-tuple-element.16), channel_id=1, source_target_pairs={{0,112},{16,0},{32,16},{48,32},{64,48},{80,64},{96,80},{112,96},{1... | collective-permute-start | bytes 32 | tf_op jit(solution)/shard_map/ppermute | solution.py:24
  13.1 0.0 copy-start
  13.8 0.0 copy-done
  13.8 0.1 fusion.6
  13.9 0.1 pad_maximum_fusion.1
  14.0 0.1 dynamic_slice.3
  14.0 0.1 broadcast_in_dim.9
  14.1 0.1 copy.7
  14.2 0.1 collective-permute-done
  14.3 0.0 collective-permute-done.1
  14.4 0.1 broadcast_compare_fusion
  14.4 6.4 %all-to-all-done = f32[16,4,16,128]{3,2,1,0:T(8,128)S(1)} async-done(((f32[16,4,16,128]{3,2,1,0:T(8,128)}), f32[16,4,16,128]{3,2,1,0:T(8,128)S(1)}, u32[]{:S(2)}, u32[]{:S(2)}) %all-to-all-start) | async-done | bytes 524320 | tf_op jit(solution)/shard_map/all_to_all | solution.py:455
  20.9 3.0 %collective-permute-start.3 = (f32[16,4,2,128]{3,2,1,0:T(2,128)S(1)}, f32[16,4,2,128]{3,2,1,0:T(2,128)S(1)}, u32[]{:S(2)}, u32[]{:S(2)}) collective-permute-start(f32[16,4,2,128]{3,2,1,0:T(2,128)S(1)} %get-tuple-element.11), channel_id=1, source_target_pairs={{0,112},{16,0},{32,16},{48,32},{64,48},{80,64},{96,80},{112,96},{1... | collective-permute-start | bytes 196616 | tf_op jit(solution)/shard_map/ppermute | solution.py:24
  23.9 0.0 collective-permute-start.2
  23.9 0.1 add_select_fusion.shift_tiles
  24.0 3.0 %turn_own.1 = (f32[16,88,128]{2,1,0:T(8,128)}, f32[8,16,128]{2,1,0:T(8,128)S(1)}) custom-call(s32[16]{0:T(128)S(1)} %and_select_fusion.shifts, f32[16,64,128]{2,1,0:T(8,128)S(1)} %bitcast.22), custom_call_target="tpu_custom_call" | custom-call | flops 4000000 | bytes 4000000 | tf_op jit(solution)/shard_map/turn_own/pallas_call | solution.py:471
  27.0 0.0 collective-permute-done.3
  27.0 2.1 %collective-permute-done.2 = f32[16,4,2,128]{3,2,1,0:T(2,128)S(1)} collective-permute-done((f32[16,4,2,128]{3,2,1,0:T(2,128)S(1)}, f32[16,4,2,128]{3,2,1,0:T(2,128)S(1)}, u32[]{:S(2)}, u32[]{:S(2)}) %collective-permute-start.2) | collective-permute-done | bytes 65568 | tf_op jit(solution)/shard_map/ppermute | solution.py:24
  29.1 0.9 %turn_ghost.1 = f32[16,88,128]{2,1,0:T(8,128)} custom-call(s32[4,128]{1,0:T(4,128)S(1)} %add_select_fusion.shift_tiles, f32[16,8,128]{2,1,0:T(8,128)S(1)} %bitcast.24, f32[16,8,128]{2,1,0:T(8,128)S(1)} %bitcast.23, f32[8,16,128]{2,1,0:T(8,128)S(1)} %get-tuple-element.7.strips_in, f32[16,88,128]{2,1,0:T(8,128)} %get-tuple-element.8.chunk), custom_call_target="tpu_custom_call", output_to_operand_aliasing={{}: (4, {})} | custom-call | tf_op jit(solution)/shard_map/turn_ghost/pallas_call | solution.py:474
  30.0 5.9 %all-to-all-start.1 = ((f32[16,88,128]{2,1,0:T(8,128)}), f32[16,88,128]{2,1,0:T(8,128)S(1)}, u32[]{:S(2)}, u32[]{:S(2)}) async-start(f32[16,88,128]{2,1,0:T(8,128)} %turn_ghost.1), calls=%async_computation.1 | async-start | bytes 1441792 | tf_op jit(solution)/shard_map/all_to_all | solution.py:481
  35.9 0.1 broadcast_bitcast_fusion
  36.0 0.1 reshape.31
  36.1 0.1 slice_bitcast_fusion.2
  36.2 0.1 maximum_bitcast_fusion
  36.2 0.1 pad_maximum_fusion
  36.3 13.4 %all-to-all-done.1 = f32[16,88,128]{2,1,0:T(8,128)S(1)} async-done(((f32[16,88,128]{2,1,0:T(8,128)}), f32[16,88,128]{2,1,0:T(8,128)S(1)}, u32[]{:S(2)}, u32[]{:S(2)}) %all-to-all-start.1) | async-done | bytes 720928 | tf_op jit(solution)/shard_map/all_to_all | solution.py:481
  49.8 2.9 %two_sections.1 = f32[64,16,128]{2,1,0:T(8,128)} custom-call(f32[24,8,128]{2,1,0:T(8,128)S(1)} %broadcast_in_dim.11.drift_rows, f32[1408,128]{1,0:T(8,128)S(1)} %bitcast.21), custom_call_target="tpu_custom_call" | custom-call | tf_op jit(solution)/shard_map/two_sections/pallas_call | solution.py:484
  (9 shorter events, 0.1 us)
Async XLA Ops:
  0.0 9.4 %copy-start.1 = (s32[16]{0:T(128)S(1)}, s32[16]{0:T(128)}, u32[]{:S(2)}) copy-start(s32[16]{0:T(128)} %param.6) | copy-start | bytes 196
  0.0 20.8 %all-to-all-start = ((f32[16,4,16,128]{3,2,1,0:T(8,128)}), f32[16,4,16,128]{3,2,1,0:T(8,128)S(1)}, u32[]{:S(2)}, u32[]{:S(2)}) async-start(f32[16,4,16,128]{3,2,1,0:T(8,128)} %bitcast.25), calls=%async_computation | async-start | bytes 1048576 | tf_op jit(solution)/shard_map/all_to_all | solution.py:455
  9.5 4.8 %collective-permute-start = (s32[2]{0:T(128)S(1)}, s32[2]{0:T(128)S(1)}, u32[]{:S(2)}, u32[]{:S(2)}) collective-permute-start(s32[2]{0:T(128)S(1)} %get-tuple-element.15), channel_id=1, source_target_pairs={{0,16},{16,32},{32,48},{48,64},{64,80},{80,96},{96,112},{112,0},{1... | collective-permute-start | bytes 32 | tf_op jit(solution)/shard_map/ppermute | solution.py:24
  10.3 4.1 %collective-permute-start.1 = (s32[2]{0:T(128)S(1)}, s32[2]{0:T(128)S(1)}, u32[]{:S(2)}, u32[]{:S(2)}) collective-permute-start(s32[2]{0:T(128)S(1)} %get-tuple-element.16), channel_id=1, source_target_pairs={{0,112},{16,0},{32,16},{48,32},{64,48},{80,64},{96,80},{112,96},{1... | collective-permute-start | bytes 32 | tf_op jit(solution)/shard_map/ppermute | solution.py:24
  13.1 0.7 %copy-start = (f32[128]{0:T(128)S(1)}, f32[128]{0:T(128)}, u32[]{:S(2)}) copy-start(f32[128]{0:T(128)} %param.5) | copy-start | bytes 1540
  20.9 6.1 %collective-permute-start.3 = (f32[16,4,2,128]{3,2,1,0:T(2,128)S(1)}, f32[16,4,2,128]{3,2,1,0:T(2,128)S(1)}, u32[]{:S(2)}, u32[]{:S(2)}) collective-permute-start(f32[16,4,2,128]{3,2,1,0:T(2,128)S(1)} %get-tuple-element.11), channel_id=1, source_target_pairs={{0,112},{16,0},{32,16},{48,32},{64,48},{80,64},{96,80},{112,96},{1... | collective-permute-start | bytes 196616 | tf_op jit(solution)/shard_map/ppermute | solution.py:24
  23.9 5.2 %collective-permute-start.2 = (f32[16,4,2,128]{3,2,1,0:T(2,128)S(1)}, f32[16,4,2,128]{3,2,1,0:T(2,128)S(1)}, u32[]{:S(2)}, u32[]{:S(2)}) collective-permute-start(f32[16,4,2,128]{3,2,1,0:T(2,128)S(1)} %get-tuple-element.12), channel_id=1, source_target_pairs={{0,16},{16,32},{32,48},{48,64},{64,80},{80,96},{96,112},{112,0},{1... | collective-permute-start | bytes 196616 | tf_op jit(solution)/shard_map/ppermute | solution.py:24
  30.0 19.7 %all-to-all-start.1 = ((f32[16,88,128]{2,1,0:T(8,128)}), f32[16,88,128]{2,1,0:T(8,128)S(1)}, u32[]{:S(2)}, u32[]{:S(2)}) async-start(f32[16,88,128]{2,1,0:T(8,128)} %turn_ghost.1), calls=%async_computation.1 | async-start | bytes 1441792 | tf_op jit(solution)/shard_map/all_to_all | solution.py:481
